TPU v7x, 32 devices: a whole 2x2x4 slice. The times are simulated.
32 devices in a mesh: dp: 16 (over z, x, core), mp: 2 (over y).
Axes of the slice: x: 2, y: 2, z: 4, core: 2. Of those that a mesh axis runs over, the one named last changes fastest.
Arguments:
- tokens: bfloat16 [4, 384, 15, 1024], P(None, 'dp'), may hold values from -6 to 6
- cotangent: bfloat16 [4, 384, 15, 1024], P(None, 'dp'), may hold values from -6 to 6
- domain_ids: int32 [4, 384], P(None, 'dp'), may hold values from 0 to 6
- domain_counts: int32 [7], replicated, may hold values from 32 to 2047
- w_query: bfloat16 [1024, 1024], P('dp', 'mp'), may hold values from -0.25 to 0.25
- w_key: bfloat16 [1024, 1024], P('dp', 'mp'), may hold values from -0.25 to 0.25
- w_value: bfloat16 [1024, 1024], P('dp', 'mp'), may hold values from -0.1875 to 0.1875
- w_out: bfloat16 [1024, 1024], P('dp', 'mp'), may hold values from -0.375 to 0.375
- w_up: bfloat16 [1024, 2048], P('dp', 'mp'), may hold values from -0.1875 to 0.1875
- w_down: bfloat16 [1024, 2048], P('dp', 'mp'), may hold values from -0.125 to 0.125
- gain_attn: bfloat16 [1024], P('dp'), may hold values from 0.5 to 1.5
- shift_attn: bfloat16 [1024], P('dp'), may hold values from -3 to 3
- gain_ffn: bfloat16 [1024], P('dp'), may hold values from 0.5 to 1.5
- shift_ffn: bfloat16 [1024], P('dp'), may hold values from -3 to 3
Outputs:
- block_out: bfloat16 [4, 384, 15, 1024], P(None, 'dp')
- grad_tokens: float32 [4, 384, 15, 1024], P(None, 'dp')
- grad_query: float32 [1024, 1024], P('dp', 'mp')
- grad_key: float32 [1024, 1024], P('dp', 'mp')
- grad_value: float32 [1024, 1024], P('dp', 'mp')
- grad_out: float32 [1024, 1024], P('dp', 'mp')
- grad_up: float32 [1024, 2048], P('dp', 'mp')
- grad_down: float32 [1024, 2048], P('dp', 'mp')
- grad_gain_attn: float32 [1024], P('dp')
- grad_shift_attn: float32 [1024], P('dp')
- grad_gain_ffn: float32 [1024], P('dp')
- grad_shift_ffn: float32 [1024], P('dp')
All inputs are finite; a program needn't handle non-finite values.
Results may differ from a plain program's by a relative error of at most 0.013.
Values may be sent and summed in bfloat16 or wider, within the bound.
A program may use at most 192 MiB of HBM per device.

v0:
```python
import functools

import jax
import jax.numpy as jnp
from jax import lax
from jax.experimental import pallas as pl
from jax.experimental.pallas import tpu as pltpu
from jax.sharding import PartitionSpec as P

BF = jnp.bfloat16
F32 = jnp.float32
HD = 128
SEG = 512
TILE = 128
PAD = 16
EPS = 1e-05
MESH = pl.DeviceIdType.MESH
VMEM_LIMIT = 62 * 1024 * 1024

Q, K, V, O, U0, U1, D0, D1 = range(8)
UPS = (U0, U1)
DOWNS = (D0, D1)
ORDERS = ("zyx", "xyz", "zxy", "zyx", "zxy", "yxz", "zyx", "yxz")
BACK_ORDERS = ("xzy", "xzy", "yxz", "zxy", "yzx", "xyz", "zxy", "xyz")

FORWARD_PLAN = (
    2, 1, 8, 4, 5, 6, 2, 8, 0, -1, 2, 4, 2, 0, 1, 3, 0, 4, 6, 3, 7, 8, 1, 5,
    0, 2, 8, 4, 0, 3, 3, 1, 8, -1, 6, 6, 1, 5, -1, 7, 2, 4, 0, 3, 1, -1, -1, 5,
    -1, -1, 7, -1, 3, 6, 5, -1, -1, 7, 4, -1, -1, 5, -1, 6, 7, -1, -1, 7, -1, -1, -1,
)
FEED_PLAN = (
    2, -1, 0, -1, -1, 1, 2, 0, 1, -1, 2, -1, 0, -1, -1, -1, 0, 1, -1, 2, -1, 0, 1, -1,
    1, 0, -1, 1, -1, 0, 1,
)
ATTN_PLAN = (
    0, 2, -1, 1, -1, 1, 0, -1, -1, 2, -1, 3, -1, 1, -1, 5, 2, 3, -1, 5, 0, -1, -1, 2,
    -1, 7, 4, 3, 6, 6, 1, 7, 4, 6, 5, 7, 0, 2, 1, 1, 7, 3, 3, 0, 4, 4, 6, 5,
    2, 4, 0, 5, 1, 6, 4, 3, 5, 0, 4, 2, 6, 5, 3,
)
GRADS_FIRST = 3


def nn(a, b):
    return lax.dot_general(a, b, (((1,), (0,)), ((), ())), preferred_element_type=F32)


def nt(a, b):
    return lax.dot_general(a, b, (((1,), (1,)), ((), ())), preferred_element_type=F32)


def flat(value):
    return value.reshape(-1, value.shape[-1])


def norm_stats(values):
    mean = jnp.mean(values, axis=-1, keepdims=True)
    center = values - mean
    inverse = lax.rsqrt(jnp.mean(center * center, axis=-1, keepdims=True) + EPS)
    return center * inverse, inverse


def norm_pull(grad, values, gain):
    normal, inverse = norm_stats(values)
    scaled = grad * gain
    first = jnp.mean(scaled, axis=-1, keepdims=True)
    second = jnp.mean(scaled * normal, axis=-1, keepdims=True)
    return inverse * (scaled - first - normal * second), normal


def fold_rows(values):
    rows, width = values.shape
    return jnp.sum(values.reshape(rows // 8, 8, width), axis=0)


def score_mask():
    row = lax.broadcasted_iota(jnp.int32, (TILE, TILE), 0)
    col = lax.broadcasted_iota(jnp.int32, (TILE, TILE), 1)
    return (row // PAD == col // PAD) & (col <= row)


def row_loop(rows, body, first=0):
    def once(index, carry):
        index = first + index
        body(pl.ds(pl.multiple_of(index * TILE, TILE), TILE), index)
        return carry

    lax.fori_loop(0, rows // TILE, once, 0)


def half_loop(count, body):
    def once(index, carry):
        body(index)
        return carry

    lax.fori_loop(0, count, once, 0)


def half(index):
    return pl.ds(pl.multiple_of(index * SEG, SEG), SEG)


def spread_rows(patches, series):
    row = lax.broadcasted_iota(jnp.int32, (series * PAD, patches * series), 0)
    col = lax.broadcasted_iota(jnp.int32, (series * PAD, patches * series), 1)
    hit = (lax.rem(row, PAD) * series + lax.div(row, PAD) == col) & (lax.rem(row, PAD) < patches)
    return jnp.where(hit, 1.0, 0.0).astype(BF)


def gather_rows(patches, series):
    row = lax.broadcasted_iota(jnp.int32, (patches * series, series * PAD), 0)
    col = lax.broadcasted_iota(jnp.int32, (patches * series, series * PAD), 1)
    return jnp.where(lax.rem(row, series) * PAD + lax.div(row, series) == col, 1.0, 0.0).astype(BF)


def to_rows(raw, target):
    micro, patches, series, _ = raw.shape
    matrix = spread_rows(patches, series)
    for part in range(micro):
        target[part * series * PAD : (part + 1) * series * PAD, :] = nn(matrix, flat(raw[part])).astype(BF)


def from_rows(source, raw):
    micro, patches, series, width = raw.shape
    matrix = gather_rows(patches, series)
    for part in range(micro):
        rows = source[part * series * PAD : (part + 1) * series * PAD, :]
        raw[part] = nn(matrix, rows).astype(raw.dtype).reshape(patches, series, width)


def norm_in(x, normed, gain, shift):
    def block(rows, _):
        normal, _inv = norm_stats(x[rows, :].astype(F32))
        normed[rows, :] = (normal * gain + shift).astype(BF)

    row_loop(x.shape[0], block)


def project(source, weights, seg, target):
    def one(m):
        target[:, half(m)] = nn(source[...], flat(weights[seg, m])).astype(BF)

    half_loop(weights.shape[1], one)


def attend(queries, keys, values, probs, mixture, first, count):
    mask = score_mask()
    scale = HD ** (-0.5)

    def group(rows, index):
        for head in range(queries.shape[1] // HD):
            cols = slice(head * HD, (head + 1) * HD)
            scores = nt(queries[rows, cols], keys[rows, cols]) * scale
            scores = jnp.where(mask, scores, -1e30)
            powers = jnp.exp(scores - jnp.max(scores, axis=-1, keepdims=True))
            share = powers * (1.0 / jnp.sum(powers, axis=-1, keepdims=True))
            probs[rows, cols] = share
            mixture[rows, cols] = nn(share.astype(BF), values[rows, cols]).astype(BF)

    row_loop(count * TILE, group, first)


def attend_back(queries, keys, values, probs, grad_mix, grad_q, grad_k, grad_v, first, count):
    scale = HD ** (-0.5)

    def group(rows, index):
        for head in range(queries.shape[1] // HD):
            cols = slice(head * HD, (head + 1) * HD)
            share = probs[rows, cols]
            grad = grad_mix[rows, cols]
            grad_share = nt(grad, values[rows, cols])
            grad_v[rows, cols] = nn(share.T.astype(BF), grad).astype(BF)
            inner = jnp.sum(grad_share * share, axis=-1, keepdims=True)
            grad_scores = share * (grad_share - inner)
            low = grad_scores.astype(BF)
            grad_q[rows, cols] = (nn(low, keys[rows, cols]) * scale).astype(BF)
            turned = grad_scores.T.astype(BF)
            grad_k[rows, cols] = (nn(turned, queries[rows, cols]) * scale).astype(BF)

    row_loop(count * TILE, group, first)


def back_through(source, weights, seg, total):
    def one(m):
        total[...] += nt(source(m), flat(weights[seg, m]))

    half_loop(weights.shape[1], one)


def feed_up(normed_two, weights, which, m, active, slope):
    hidden = nn(normed_two[...], flat(weights[UPS[which], m]))
    bell = 0.5 + 0.5 * lax.erf(hidden * (0.5**0.5))
    active[which, m] = (hidden * bell).astype(BF)
    density = jnp.exp(-0.5 * hidden * hidden) * 0.3989422804014327
    slope[which, m] = bell + hidden * density


def turn(source, target):
    def block(rows, _):
        target[:, rows] = source[rows, :].T

    row_loop(source.shape[0], block)


def weight_grad(turned, right, target, seg):
    def one(m):
        product = nn(turned[...], right(m)).astype(BF)
        target[seg, m] = product.reshape(target.shape[2:])

    half_loop(target.shape[1], one)


class Place:
    def __init__(self, shape):
        self.nz, self.nx, self.ny = shape
        index = lax.axis_index("dp")
        self.core = lax.rem(index, 2)
        chip = lax.div(index, 2)
        self.at = {"z": lax.div(chip, self.nx), "x": lax.rem(chip, self.nx), "y": lax.axis_index("mp")}
        self.count = {"z": self.nz, "x": self.nx, "y": self.ny}

    def device(self, core=None, **moved):
        at = {**self.at, **moved}
        core = self.core if core is None else core
        return ((at["z"] * self.nx + at["x"]) * 2 + core, at["y"])

    def partner(self):
        return self.device(core=1 - self.core)

    def neighbour(self, dim, step):
        return self.device(**{dim: self.at[dim] + step})

    def barrier(self, dims):
        semaphore = pltpu.get_barrier_semaphore()
        pl.semaphore_signal(semaphore, inc=1, device_id=self.partner(), device_id_type=MESH)
        peers = 1
        for dim in dims:
            for step in (1, -1):
                there = self.at[dim] + step
                valid = (there >= 0) & (there < self.count[dim])
                peers = peers + valid.astype(jnp.int32)

                @pl.when(valid)
                def _(dim=dim, step=step):
                    other = self.neighbour(dim, step)
                    pl.semaphore_signal(semaphore, inc=1, device_id=other, device_id_type=MESH)

        pl.semaphore_wait(semaphore, peers)


def link_slots(count, dims):
    return sum(2 * (count[dim] - 1) for dim in dims)


class Gather:
    def __init__(self, place, buffer, axes, order, sems):
        self.place, self.buffer, self.axes, self.order = place, buffer, axes, order
        self.send, self.recv, self.pass_send, self.pass_recv = sems
        self.rounds = [(dim, t) for dim in order for t in range(place.count[dim] - 1)]
        self.slots = {}
        for dim, t in self.rounds:
            for way in (1, -1):
                self.slots[dim, t, way] = len(self.slots)

    def block(self, dim, position, core):
        done = self.order[: self.order.index(dim)] if dim else ""
        index = []
        for axis in self.axes:
            if axis == dim:
                index.append(position)
            elif axis in done:
                index.append(pl.ds(0, self.place.count[axis]))
            else:
                index.append(self.place.at[axis])
        return self.buffer.at[tuple(index) + (core,)]

    def link(self, dim, t, way, position, device):
        block = self.block(dim, position, self.place.core)
        slot = self.slots[dim, t, way]
        return pltpu.make_async_remote_copy(
            block, block, self.send.at[slot], self.recv.at[slot], device_id=device, device_id_type=MESH
        )

    def hand(self, slot, dim, position, core):
        block = self.block(dim, position, core)
        return pltpu.make_async_remote_copy(
            block,
            block,
            self.pass_send.at[slot],
            self.pass_recv.at[slot],
            device_id=self.place.partner(),
            device_id_type=MESH,
        )

    def sends(self, dim, t):
        here, count = self.place.at[dim], self.place.count[dim]
        yield 1, here - t, (here - t >= 0) & (here < count - 1)
        yield -1, here + t, (here + t < count) & (here > 0)

    def arrivals(self, dim, t):
        here, count = self.place.at[dim], self.place.count[dim]
        yield 1, here - 1 - t, here - 1 - t >= 0
        yield -1, here + 1 + t, here + 1 + t < count

    def start(self):
        self.hand(len(self.slots), "", None, self.place.core).start()
        self.send_round(0)

    def send_round(self, number):
        dim, t = self.rounds[number]
        for way, position, valid in self.sends(dim, t):

            @pl.when(valid)
            def _(way=way, position=position):
                self.link(dim, t, way, position, self.place.neighbour(dim, way)).start()

    def advance(self, number):
        dim, t = self.rounds[number - 1]
        for way, position, valid in self.arrivals(dim, t):

            @pl.when(valid)
            def _(way=way, position=position):
                self.link(dim, t, way, position, self.place.partner()).wait_recv()
                self.hand(self.slots[dim, t, way], dim, position, self.place.core).start()

        if number < len(self.rounds):
            self.send_round(number)

    def steps(self):
        return [self.start] + [functools.partial(self.advance, n + 1) for n in range(len(self.rounds))]

    def finish(self):
        other = 1 - self.place.core
        self.hand(len(self.slots), "", None, other).wait_recv()
        for dim, t in self.rounds:
            for way, position, valid in self.arrivals(dim, t):

                @pl.when(valid)
                def _(dim=dim, t=t, way=way, position=position):
                    self.hand(self.slots[dim, t, way], dim, position, other).wait_recv()

    def drain(self):
        self.hand(len(self.slots), "", None, self.place.core).wait_send()
        for dim, t in self.rounds:
            for way, position, valid in self.sends(dim, t):

                @pl.when(valid)
                def _(dim=dim, t=t, way=way, position=position):
                    self.link(dim, t, way, position, self.place.partner()).wait_send()

            for way, position, valid in self.arrivals(dim, t):

                @pl.when(valid)
                def _(dim=dim, t=t, way=way, position=position):
                    self.hand(self.slots[dim, t, way], dim, position, self.place.core).wait_send()


class Scatter:
    def __init__(self, place, mine, axes, order, inbox, hand_box, sems, both=False):
        self.place, self.mine, self.axes, self.order, self.both = place, mine, axes, order, both
        self.inbox, self.hand_box = inbox, hand_box
        self.send, self.recv = sems
        self.rounds = [(dim, t) for dim in order for t in range(place.count[dim] - 1)]
        self.slots = {}
        for dim, t in self.rounds:
            for way in (1, -1):
                self.slots[dim, t, way] = len(self.slots) + 1

    def own(self, index):
        return index + ((() if self.both else (self.place.core,)))

    def hand(self):
        whole = tuple(pl.ds(0, self.place.count[axis]) for axis in self.axes)
        source = self.mine.at[whole] if self.both else self.mine.at[whole + (1 - self.place.core,)]
        return pltpu.make_async_remote_copy(
            source, self.hand_box, self.send.at[0], self.recv.at[0], device_id=self.place.partner(), device_id_type=MESH
        )

    def start(self):
        self.hand().start()

    def take_hand(self):
        self.hand().wait_recv()
        first = self.place.count[self.axes[0]]
        rest = tuple(pl.ds(0, self.place.count[axis]) for axis in self.axes[1:])
        if self.both:
            self.hand().wait_send()
            self.mine[...] = self.mine[...] + self.hand_box[...]
        else:
            for p in range(first):
                for r in range(self.place.count[self.axes[1]]):
                    index = (p, r) + rest[1:]
                    here = self.mine[index + (self.place.core,)].astype(F32)
                    there = self.hand_box[index].astype(F32)
                    self.mine[index + (self.place.core,)] = (here + there).astype(self.mine.dtype)
        self.send_round(0)

    def block(self, dim, position):
        done = self.order[: self.order.index(dim)]
        index = []
        for axis in self.axes:
            if axis == dim:
                index.append(position)
            elif axis in done:
                index.append(self.place.at[axis])
            else:
                index.append(pl.ds(0, self.place.count[axis]))
        return self.own(tuple(index))

    def link(self, dim, t, way, position, device):
        slot = self.slots[dim, t, way]
        return pltpu.make_async_remote_copy(
            self.mine.at[self.block(dim, position)],
            self.inbox[slot],
            self.send.at[slot],
            self.recv.at[slot],
            device_id=device,
            device_id_type=MESH,
        )

    def sends(self, dim, t):
        here, count = self.place.at[dim], self.place.count[dim]
        yield 1, count - 1 - t + here, (t >= here) & (here < count - 1)
        back = count - 1 - here
        yield -1, t - back, (t >= back) & (here > 0)

    def arrivals(self, dim, t):
        here, count = self.place.at[dim], self.place.count[dim]
        yield 1, count - 2 - t + here, (t >= here - 1) & (here > 0)
        back = count - 1 - here
        yield -1, t + 1 - back, (t >= back - 1) & (here < count - 1)

    def send_round(self, number):
        dim, t = self.rounds[number]
        for way, position, valid in self.sends(dim, t):

            @pl.when(valid)
            def _(way=way, position=position):
                self.link(dim, t, way, position, self.place.neighbour(dim, way)).start()

    def advance(self, number):
        dim, t = self.rounds[number - 1]
        for way, position, valid in self.arrivals(dim, t):

            @pl.when(valid)
            def _(way=way, position=position):
                self.link(dim, t, way, position, self.place.partner()).wait_recv()
                index = self.block(dim, position)
                total = self.mine[index].astype(F32) + self.inbox[self.slots[dim, t, way]][...].astype(F32)
                self.mine[index] = total.astype(self.mine.dtype)

        if number < len(self.rounds):
            self.send_round(number)

    def steps(self):
        later = [functools.partial(self.advance, n + 1) for n in range(len(self.rounds))]
        return [self.start, self.take_hand] + later

    def result(self):
        return self.mine[self.own(tuple(self.place.at[axis] for axis in self.axes))]

    def drain(self):
        if not self.both:
            self.hand().wait_send()
        for dim, t in self.rounds:
            for way, position, valid in self.sends(dim, t):

                @pl.when(valid)
                def _(dim=dim, t=t, way=way, position=position):
                    self.link(dim, t, way, position, self.place.partner()).wait_send()


def inbox_shapes(count, axes, order, block):
    shapes, slots, left = [], {}, dict(count)
    for dim in order:
        left.pop(dim)
        for t in range(count[dim] - 1):
            for way in (1, -1):
                if way == 1 or count[dim] > 2:
                    shapes.append(tuple(count[axis] for axis in axes if axis in left) + block)
                slots[dim, t, way] = len(shapes) - 1
    return shapes, slots


def open_inbox(run, count, axes, order, block, boxes):
    shapes, slots = inbox_shapes(count, axes, order, block)
    for key, slot in run.slots.items():
        run.inbox[slot] = boxes[slots[key]]
    del boxes[: len(shapes)]


def play(plan, comm, pieces):
    plan = list(plan)
    while plan:
        token = plan.pop(0)
        if token >= 0:
            if comm:
                comm[token].pop(0)()
        elif callable(pieces[0]):
            pieces.pop(0)()
        else:
            count, piece = pieces.pop(0)
            between = [[] for _ in range(count - 1)]
            for spot in range(count - 1):
                while plan[0] >= 0:
                    token = plan.pop(0)
                    if comm:
                        between[spot].append(comm[token].pop(0))
                plan.pop(0)

            def once(index, carry, piece=piece, between=between):
                piece(index)
                for spot, steps in enumerate(between):
                    if steps:

                        @pl.when(index == spot)
                        def _(steps=steps):
                            for step in steps:
                                step()

                return carry

            lax.fori_loop(0, count, once, 0)
    assert not pieces and not any(comm.values())


class Mover:
    def __init__(self, sems):
        self.sems, self.used, self.open = sems, 0, []

    def start(self, source, target):
        copy = pltpu.make_async_copy(source, target, self.sems.at[self.used])
        self.used += 1
        copy.start()
        return copy

    def save(self, source, target):
        self.open.append(self.start(source, target))

    def close(self):
        for copy in self.open:
            copy.wait()


def read_vectors(vectors, tiles):
    nz, nx = tiles.shape[:2]
    pieces = [tiles[z, x, 0] + tiles[z, x, 1] for z in range(nz) for x in range(nx)]
    vectors[...] = jnp.concatenate(pieces, axis=1)


def column_parts(weights):
    wq, wk, wv, wo, wu, wd = weights
    left, right = pl.ds(0, SEG), pl.ds(SEG, SEG)
    return [wq, wk, wv, wo, wu.at[:, left], wu.at[:, right], wd.at[:, left], wd.at[:, right]]


def fill_tile(place, tiles, norms):
    tile = (place.at["z"], place.at["x"], place.core)
    tiles[tile] = jnp.zeros(tiles.shape[3:], F32)
    share = norms[0].shape[1]
    for line, norm in enumerate(norms):
        value = norm[...].astype(F32)
        for core in range(2):

            @pl.when(place.core == core)
            def _(line=line, value=value, core=core):
                tiles[tile + (slice(line, line + 1), slice(core * share, (core + 1) * share))] = value


FWD_OUT = (
    "x", "q", "k", "v", "probs", "mix", "res", "nrm2", "active", "slope", "out", "cot", "gl", "glt", "weight",
    "nrmt",
)
KEPT = len(FWD_OUT)


def forward_kernel(shape, micro, tokens, cotangent, ids, counts, *refs):
    if shape:
        weights, norms, g_out, refs = refs[:6], refs[6:10], refs[10], refs[11:]
    else:
        g_in, vectors_in, refs = refs[0], refs[1], refs[2:]
    if shape:
        vectors, refs = refs[0], refs[1:]
    else:
        vectors = vectors_in
    saved = dict(zip(FWD_OUT, refs[:KEPT]))
    here = dict(zip(FWD_OUT, refs[KEPT : 2 * KEPT]))
    refs = refs[2 * KEPT :]
    raw, nrm, low, total, g, sems = refs[:6]
    mover = Mover(sems)
    y = lax.axis_index("mp")
    take = mover.start(tokens.at[pl.ds(y * micro, micro)], raw)
    x, q, k, v, probs, mix, res, nrm2, active, slope, out, cot, gl, glt, weight, nrmt = (
        here[name] for name in FWD_OUT
    )

    def keep(*names):
        for name in names:
            mover.save(here[name], saved[name])

    comm = {}
    if shape:
        tiles, send, recv, pass_send, pass_recv = refs[6:]
        place = Place(shape)
        spot = (place.at["y"], place.at["z"], place.at["x"], place.core)
        mine = [mover.start(part, g.at[(seg,) + spot]) for seg, part in enumerate(column_parts(weights))]
        fill_tile(place, tiles, norms)
        place.barrier("zxy")
        pick = lambda seg: tuple(sem.at[seg] for sem in (send, recv, pass_send, pass_recv))
        runs = [Gather(place, g.at[seg], "yzx", ORDERS[seg], pick(seg)) for seg in range(8)]
        runs.append(Gather(place, tiles, "zx", "zx", pick(8)))
        comm = {seg: run.steps() for seg, run in enumerate(runs)}
        for seg in range(8):
            comm[seg][0] = lambda seg=seg: (mine[seg].wait(), runs[seg].start())

        def have(seg):
            runs[seg].finish()
            if seg < 8:
                mover.save(g.at[seg], g_out.at[seg])
            else:
                read_vectors(vectors, tiles)

    else:
        loads = [mover.start(g_in.at[seg], g.at[seg]) for seg in range(8)]

        def have(seg):
            if seg < 8:
                loads[seg].wait()

    def spread():
        take.wait()
        to_rows(raw, x)
        keep("x")
        loads_cot.append(mover.start(cotangent.at[pl.ds(y * micro, micro)], raw))
        row_weights(ids, counts, y, micro, weight)

    loads_cot = []

    def weigh():
        loads_cot[0].wait()
        to_rows(raw, cot)

        def block(rows, _):
            gl[rows, :] = (cot[rows, :].astype(F32) * weight[rows, :]).astype(BF)

        row_loop(cot.shape[0], block)
        turn(gl, glt)
        keep("cot", "gl", "glt", "weight")

    def norm_one():
        have(8)
        norm_in(x, nrm, vectors[0:1, :], vectors[1:2, :])
        turn(nrm, nrmt)
        keep("nrmt")

    def head_part(seg, target, name):
        have(seg)
        project(nrm, g, seg, target)
        keep(name)

    third = x.shape[0] // TILE // 3

    def mixing(part):
        attend(q, k, v, probs, mix, part * third, third)

    def project_out():
        keep("probs", "mix")
        have(O)
        res[...] = x[...].astype(F32)
        back_through(lambda m: mix[:, half(m)], g, O, res)
        keep("res")

    def norm_two():
        gain, shift = vectors[2:3, :], vectors[3:4, :]

        def block(rows, _):
            normal, _inv = norm_stats(res[rows, :])
            nrm2[rows, :] = (normal * gain + shift).astype(BF)

        row_loop(x.shape[0], block)
        keep("nrm2")

    def up(which, m):
        if m == 0:
            have(UPS[which])
        feed_up(nrm2, g, which, m, active, slope)
        mover.save(active.at[which, m], saved["active"].at[which, m])
        mover.save(slope.at[which, m], saved["slope"].at[which, m])

    def down(which):
        have(DOWNS[which])
        if which == 0:
            total[...] = res[...]
        back_through(lambda m: active[which, m], g, DOWNS[which], total)

    def last():
        low[...] = total[...].astype(BF)
        from_rows(low, out)
        keep("out")

    pieces = [spread, weigh, norm_one]
    pieces += [functools.partial(head_part, *args) for args in ((Q, q, "q"), (K, k, "k"), (V, v, "v"))]
    pieces += [(3, mixing), project_out, norm_two]
    pieces += [functools.partial(up, which, m) for which in range(2) for m in range(2)]
    pieces += [functools.partial(down, which) for which in range(2)] + [last]
    play(FORWARD_PLAN, comm, pieces)
    if shape:
        for run in runs:
            run.drain()
    mover.close()


def row_weights(ids, counts, y, micro, target):
    series = ids.shape[1]
    sums = counts[0]
    for kind in range(1, counts.shape[0]):
        sums = sums + counts[kind]
    mean = jnp.full((PAD, 1), sums.astype(F32), F32) / counts.shape[0]

    def one(index, carry):
        kind = ids[y * micro + lax.div(index, series), lax.rem(index, series)]
        count = counts[kind].astype(F32)
        target[pl.ds(pl.multiple_of(index * PAD, PAD), PAD), :] = 2.0 * mean / (mean + count)
        return carry

    lax.fori_loop(0, micro * series, one, 0)


class Swap:
    def __init__(self, place, mover, sems, ready, source, target):
        self.mover, self.source, self.ready = mover, source, ready
        y, (micro, patches) = place.at["y"], source.shape[:2]
        cut = patches // 2 + 1
        self.spot = target.at[pl.ds(y * micro, micro)]
        self.copies = []
        for part in range(micro):
            for piece in (pl.ds(0, cut), pl.ds(cut, patches - cut)):
                slot = 2 * len(self.copies)
                self.copies.append(
                    pltpu.make_async_remote_copy(
                        source.at[part, piece],
                        target.at[y * micro + part, piece],
                        sems.at[slot],
                        sems.at[slot + 1],
                        device_id=place.device(y=1 - y),
                        device_id_type=MESH,
                    )
                )

    def start(self):
        self.ready()
        self.copies[0].start()
        self.mover.save(self.source, self.spot)

    def steps(self):
        return [self.start] + [copy.start for copy in self.copies[1:]]

    def wait(self):
        for copy in self.copies:
            copy.wait()


def feed_back_kernel(shape, vectors, g_in, active_in, slope_in, nrm2_in, res_in, out_in, cot_in, gl_in, glt_in, weight_in, mix_in, *refs):
    if shape:
        dw_out, gres_out, gm_out, vec, pair, grad_down, refs = refs[:6] + (refs[6:],)
    else:
        dw_out, gres_out, gm_out, vec, refs = refs[:4] + (refs[4:],)
    cot, weight, active, slope, nrm2, res, g, dw, gl, glt, gh, n2t, gn2, gres, mix, gm, sems = refs[:17]
    mover = Mover(sems)
    loads = {"glt": mover.start(glt_in, glt), ("active", 0): mover.start(active_in.at[0], active.at[0])}
    loads["gl"] = mover.start(gl_in, gl)
    for which in range(2):
        if which == 1:
            loads["active", which] = mover.start(active_in.at[which], active.at[which])
        loads["d", which] = mover.start(g_in.at[DOWNS[which]], g.at[2 + which])
        loads["slope", which] = mover.start(slope_in.at[which], slope.at[which])
    loads["nrm2"] = mover.start(nrm2_in, nrm2)
    for which in range(2):
        loads["u", which] = mover.start(g_in.at[UPS[which]], g.at[which])
    loads["res"] = mover.start(res_in, res)
    loads["cot"] = mover.start(cot_in, cot)
    loads["mix"] = mover.start(mix_in, mix)
    loads["o"] = mover.start(g_in.at[O], g.at[4])
    loads["weight"] = mover.start(weight_in, weight)
    comm = {}
    if shape:
        half_out, hands, send, recv, ysem = refs[17:22]
        boxes = list(refs[22:])
        side = mover.start(out_in, half_out)
        place = Place(shape)
        place.barrier("zxy")
        runs = []
        for which in range(2):
            order = BACK_ORDERS[DOWNS[which]]
            run = Scatter(
                place, dw.at[2 + which], "yzx", order, {}, hands.at[which], (send.at[which], recv.at[which])
            )
            open_inbox(run, place.count, "yzx", order, dw.shape[-2:], boxes)
            runs.append(run)
        swap = Swap(place, mover, ysem, side.wait, half_out, pair)
        comm = {0: runs[0].steps(), 1: runs[1].steps(), 2: swap.steps()}

    def down_grad(which):
        if which == 0:
            loads["glt"].wait()
        loads["active", which].wait()
        weight_grad(glt, lambda m: active[which, m], dw, 2 + which)
        if not shape:
            mover.save(dw.at[2 + which], dw_out.at[2 + which])

    def hidden_grad(which):
        if which == 0:
            loads["gl"].wait()
        loads["d", which].wait()
        loads["slope", which].wait()

        def one(m):
            pulled = nn(gl[...], flat(g[2 + which, m]))
            gh[which, m] = (pulled * slope[which, m]).astype(BF)

        half_loop(g.shape[1], one)

    def turn_two():
        loads["nrm2"].wait()
        turn(nrm2, n2t)
        gn2[...] = jnp.zeros_like(gn2)

    def up_grad(which):
        weight_grad(n2t, lambda m: gh[which, m], dw, which)
        mover.save(dw.at[which], dw_out.at[which])

    def norm_grad(which):
        loads["u", which].wait()
        back_through(lambda m: gh[which, m], g, which, gn2)

    def last():
        for name in ("res", "cot", "weight"):
            loads[name].wait()
        gain = vectors[2:3, :]
        vec[...] = jnp.zeros_like(vec)

        def block(rows, _):
            grad = gn2[rows, :]
            pulled, normal = norm_pull(grad, res[rows, :], gain)
            vec[0] += fold_rows(grad * normal)
            vec[1] += fold_rows(grad)
            total = cot[rows, :].astype(F32) * weight[rows, :] + pulled
            gres[rows, :] = total
            gl[rows, :] = total.astype(BF)

        row_loop(cot.shape[0], block)
        mover.save(gres, gres_out)

    def mix_grad():
        loads["o"].wait()
        project(gl, g, 4, gm)
        mover.save(gm, gm_out)

    def out_grad():
        loads["mix"].wait()
        weight_grad(glt, lambda m: mix[:, half(m)], dw, 4)
        mover.save(dw.at[4], dw_out.at[4])

    pieces = []
    for which in range(2):
        pieces += [functools.partial(down_grad, which), functools.partial(hidden_grad, which)]
    pieces.append(turn_two)
    for which in range(2):
        pieces += [functools.partial(up_grad, which), functools.partial(norm_grad, which)]
    pieces += [last, mix_grad, lambda: turn(gl, glt), out_grad]
    play(FEED_PLAN, comm, pieces)
    if shape:
        for which in range(2):
            grad_down[:, which * SEG : (which + 1) * SEG] = runs[which].result().astype(F32)
            runs[which].drain()
        swap.wait()
    mover.close()


def vector_tiles(tiles, vec_a, vec_f):
    tiles[...] = jnp.zeros_like(tiles)
    nz, nx = tiles.shape[:2]
    for line, (source, part) in enumerate(((vec_a, 0), (vec_a, 1), (vec_f, 0), (vec_f, 1))):
        row = jnp.sum(source[part], axis=0, keepdims=True)
        for z in range(nz):
            for x in range(nx):
                chip = z * nx + x
                tiles[z, x, line : line + 1, :] = row[:, chip * 128 : (chip + 1) * 128]


BACK_IN = ("gm", "q", "k", "v", "probs", "nrmt", "gres", "x")
SHARED = (U0, U1, O, Q, K, V)
KEPT_GRADS = (0, 1, 4)


def attn_back_kernel(shape, vectors, vec_f, g_in, dw_in, *refs):
    given = dict(zip(BACK_IN, refs[:8]))
    refs = refs[8:]
    if shape:
        pair, grads, vec_out, refs = refs[0], refs[1:6], refs[6], refs[7:]
    else:
        dw_out, out, vec, refs = refs[0], refs[1], refs[2], refs[3:]
    here = dict(zip(BACK_IN, refs[:8]))
    g, dw, gal, gq, gk, gv, raw, sems = refs[8:16]
    mover = Mover(sems)
    loads, comm = {}, {}
    if shape:
        held, tiles, hands, vec_hand, ybox, vec, send, recv, ysem = refs[16:25]
        boxes = list(refs[25:])
        for spot, part in enumerate(KEPT_GRADS):
            loads["dw", spot] = mover.start(dw_in.at[part], held.at[spot])
    for name in BACK_IN:
        loads[name] = mover.start(given[name], here[name])
    for seg in (Q, K, V):
        loads[seg] = mover.start(g_in.at[seg], g.at[seg])
    gm, q, k, v, probs, nrmt, gres, x = (here[name] for name in BACK_IN)
    gn = probs
    if shape:
        place = Place(shape)
        place.barrier("zxy")
        runs = []
        for spot, seg in enumerate(SHARED):
            source = held.at[spot] if spot < 3 else dw.at[seg]
            order = BACK_ORDERS[seg]
            run = Scatter(place, source, "yzx", order, {}, hands.at[spot], (send.at[spot], recv.at[spot]))
            open_inbox(run, place.count, "yzx", order, dw.shape[-2:], boxes)
            runs.append(run)
        run = Scatter(place, tiles, "zx", "zx", {}, vec_hand, (send.at[6], recv.at[6]), both=True)
        open_inbox(run, {"z": place.nz, "x": place.nx}, "zx", "zx", (8, 128), boxes)
        runs.append(run)
        swap = Swap(place, mover, ysem, lambda: None, raw, pair)
        comm = {spot: run.steps() for spot, run in enumerate(runs)}
        comm[7] = swap.steps()
        for spot in range(3):
            comm[spot][0] = lambda spot=spot: (loads["dw", spot].wait(), runs[spot].start())

    third = gal.shape[0] // TILE // 3

    def ready():
        for name in BACK_IN[:6]:
            loads[name].wait()

    def mixing(part):
        attend_back(q, k, v, probs, gm, gq, gk, gv, part * third, third)

    def head_grad(seg, grad):
        weight_grad(nrmt, lambda m: grad[:, half(m)], dw, seg)
        if not shape:
            mover.save(dw.at[seg], dw_out.at[seg])

    def norm_grad(seg, grad):
        if seg == Q:
            gn[...] = jnp.zeros_like(gn)
        loads[seg].wait()
        back_through(lambda m: grad[:, half(m)], g, seg, gn)

    def last():
        loads["gres"].wait()
        loads["x"].wait()
        gain = vectors[0:1, :]
        vec[...] = jnp.zeros_like(vec)

        def block(rows, _):
            grad = gn[rows, :]
            pulled, normal = norm_pull(grad, x[rows, :].astype(F32), gain)
            vec[0] += fold_rows(grad * normal)
            vec[1] += fold_rows(grad)
            gal[rows, :] = (gres[rows, :] + pulled).astype(BF)

        row_loop(gal.shape[0], block)
        from_rows(gal, raw)
        if shape:
            vector_tiles(tiles, vec, vec_f)
        else:
            mover.save(raw, out)

    heads = ((Q, gq), (K, gk), (V, gv))
    pieces = [ready, (3, mixing)]
    pieces += [functools.partial(head_grad, *pair_of) for pair_of in heads[:GRADS_FIRST]]
    pieces += [functools.partial(norm_grad, *pair_of) for pair_of in heads] + [last]
    pieces += [functools.partial(head_grad, *pair_of) for pair_of in heads[GRADS_FIRST:]]
    play(ATTN_PLAN, comm, pieces)
    if shape:
        here_tile = tiles.at[place.at["z"], place.at["x"]]
        copy = pltpu.make_async_remote_copy(
            here_tile, ybox, ysem.at[8], ysem.at[9], device_id=place.device(y=1 - place.at["y"]), device_id_type=MESH
        )
        copy.start()
        for spot, seg in enumerate(SHARED[2:]):
            grads[(3, 0, 1, 2)[spot]][...] = runs[2 + spot].result().astype(F32)
        for which in range(2):
            grads[4][:, which * SEG : (which + 1) * SEG] = runs[which].result().astype(F32)
        for run in runs:
            run.drain()
        copy.wait()
        vec_out[...] = tiles[place.at["z"], place.at["x"]] + ybox[...]
        swap.wait()
    mover.close()


def shape_of(shape, dtype):
    return jax.ShapeDtypeStruct(shape, dtype)


IN_VMEM = pl.BlockSpec(memory_space=pltpu.VMEM)
IN_SMEM = pl.BlockSpec(memory_space=pltpu.SMEM)
ANYWHERE = pl.BlockSpec(memory_space=pl.ANY)
DMA = pltpu.SemaphoreType.DMA


def call(body, outs, ins, out_specs, scratch, name, collective=None):
    params = {"vmem_limit_bytes": VMEM_LIMIT}
    if collective is not None:
        params.update(collective_id=collective, has_side_effects=True)
    return pl.pallas_call(
        body,
        out_shape=outs,
        in_specs=ins,
        out_specs=out_specs,
        scratch_shapes=scratch,
        compiler_params=pltpu.CompilerParams(**params),
        name=name,
    )


def vmem(like):
    return pltpu.VMEM(like.shape, like.dtype)


def forward(shape, micro, tokens, cotangent, ids, counts, weights, norms, g_in=None, vectors_in=None):
    _, patches, series, width = tokens.shape
    rows = micro * series * PAD
    full = g_in.shape if shape is None else (8, shape[2], shape[0], shape[1], 2, weights[0].shape[0], SEG)
    low, high = shape_of((rows, width), BF), shape_of((rows, width), F32)
    wide = (2, full[1], rows, SEG)
    raw = shape_of((micro, patches, series, width), BF)
    kinds = {name: low for name in FWD_OUT}
    kinds.update(
        probs=high,
        res=high,
        active=shape_of(wide, BF),
        slope=shape_of(wide, F32),
        out=raw,
        glt=shape_of((width, rows), BF),
        nrmt=shape_of((width, rows), BF),
        weight=shape_of((rows, 1), F32),
    )
    saved = tuple(kinds[name] for name in FWD_OUT)
    scratch = [vmem(kind) for kind in saved] + [vmem(raw), vmem(low), vmem(low), vmem(high), pltpu.VMEM(full, BF), DMA((64,))]
    if shape is None:
        results = call(
            functools.partial(forward_kernel, None, micro),
            saved,
            [ANYWHERE, ANYWHERE, IN_SMEM, IN_SMEM, ANYWHERE, IN_VMEM],
            (ANYWHERE,) * KEPT,
            scratch,
            "forward",
        )(tokens, cotangent, ids, counts, g_in, vectors_in)
        return g_in, vectors_in, dict(zip(FWD_OUT, results))
    count = dict(zip("zxy", shape))
    slots = link_slots(count, "zxy")
    scratch += [pltpu.VMEM(shape[:2] + (2, 8, 128), F32)]
    scratch += [DMA((9, slots)), DMA((9, slots)), DMA((9, slots + 1)), DMA((9, slots + 1))]
    results = call(
        functools.partial(forward_kernel, shape, micro),
        (shape_of(full, BF), shape_of((8, width), F32)) + saved,
        [ANYWHERE, ANYWHERE, IN_SMEM, IN_SMEM] + [ANYWHERE] * 6 + [IN_VMEM] * 4,
        (ANYWHERE, IN_VMEM) + (ANYWHERE,) * KEPT,
        scratch,
        "forward",
        0,
    )(tokens, cotangent, ids, counts, *weights, *norms)
    return results[0], results[1], dict(zip(FWD_OUT, results[2:]))


def scatter_scratch(segs, part, count, orders):
    rows, cols = part.shape[-2:]
    slots = link_slots(count, "zxy") + 1
    boxes = []
    for order in orders:
        boxes += [pltpu.VMEM(s, BF) for s in inbox_shapes(count, "yzx", order, (rows, cols))[0]]
    hands = pltpu.VMEM((len(orders),) + part.shape[1:4] + (rows, cols), BF)
    return hands, [DMA((segs, slots)), DMA((segs, slots))], boxes


def pair_of(raw, ny):
    return shape_of((ny * raw.shape[0],) + raw.shape[1:], BF)


def feed_back(shape, vectors, g, kept):
    low, high, raw = kept["x"], kept["res"], kept["out"]
    rows, width = low.shape
    part = shape_of((5,) + g.shape[1:], BF)
    turned = pltpu.VMEM((width, rows), BF)
    scratch = [
        vmem(low),
        pltpu.VMEM((rows, 1), F32),
        vmem(kept["active"]),
        vmem(kept["slope"]),
        vmem(low),
        vmem(high),
        vmem(part),
        vmem(part),
        vmem(low),
        turned,
        vmem(kept["active"]),
        turned,
        vmem(high),
        vmem(high),
        vmem(low),
        vmem(low),
        DMA((32,)),
    ]
    given = [g] + [kept[name] for name in ("active", "slope", "nrm2", "res", "out", "cot", "gl", "glt", "weight", "mix")]
    outs = [part, shape_of(high.shape, F32), shape_of(low.shape, BF), shape_of((2, 8, width), F32)]
    specs = [ANYWHERE, ANYWHERE, ANYWHERE, IN_VMEM]
    if shape:
        count = dict(zip("zxy", shape))
        hands, sems, boxes = scatter_scratch(2, part, count, [BACK_ORDERS[seg] for seg in DOWNS])
        scratch += [vmem(raw), hands] + sems + [DMA((8,))] + boxes
        outs += [pair_of(raw, shape[2]), shape_of((part.shape[-2], 2 * SEG), F32)]
        specs += [ANYWHERE, IN_VMEM]
    return call(
        functools.partial(feed_back_kernel, shape),
        tuple(outs),
        [IN_VMEM] + [ANYWHERE] * 11,
        tuple(specs),
        scratch,
        "feed_back",
        1 if shape else None,
    )(vectors, *given)


def attn_back(shape, vectors, vec_f, g, dw_in, kept):
    low, raw = kept["x"], kept["out"]
    width = low.shape[1]
    part = shape_of((3,) + g.shape[1:], BF)
    scratch = [vmem(kept[name]) for name in BACK_IN]
    scratch += [vmem(part), vmem(part), vmem(low), vmem(low), vmem(low), vmem(low), vmem(raw), DMA((32,))]
    vec = shape_of((2, 8, width), F32)
    if shape:
        nz, nx, ny = shape
        count = dict(zip("zxy", shape))
        share = part.shape[-2]
        small, large = shape_of((share, SEG), F32), shape_of((share, 2 * SEG), F32)
        outs = [pair_of(raw, ny)] + [small] * 4 + [large, shape_of((8, 128), F32)]
        specs = [ANYWHERE] + [IN_VMEM] * 6
        hands, sems, boxes = scatter_scratch(7, part, count, [BACK_ORDERS[seg] for seg in SHARED])
        tiles = pltpu.VMEM((nz, nx, 8, 128), F32)
        scratch += [vmem(part), tiles, hands, tiles, pltpu.VMEM((8, 128), F32), vmem(vec)]
        scratch += sems + [DMA((10,))] + boxes
        scratch += [pltpu.VMEM(s, F32) for s in inbox_shapes({"z": nz, "x": nx}, "zx", "zx", (8, 128))[0]]
    else:
        outs, specs = [part, raw, vec], [ANYWHERE, ANYWHERE, IN_VMEM]
        outs[1] = shape_of(raw.shape, BF)
    return call(
        functools.partial(attn_back_kernel, shape),
        tuple(outs),
        [IN_VMEM] * 2 + [ANYWHERE] * 10,
        tuple(specs),
        scratch,
        "attn_back",
        2 if shape else None,
    )(vectors, vec_f, g, dw_in, *(kept[name] for name in BACK_IN))


def chip_grid(chips):
    nx = 1
    while (nx * 2) ** 2 <= chips:
        nx *= 2
    return chips // nx, nx


def body(counts_of, tokens, cotangent, domain_ids, domain_counts, *params):
    weights, norms = params[:6], params[6:]
    n_dp, n_mp = counts_of
    micro = tokens.shape[0] // n_mp
    width = tokens.shape[3]
    share = width // n_dp
    y = lax.axis_index("mp")
    linked = n_mp == 2 and share * 2 == TILE
    flip = lambda array: jnp.transpose(array, (0, 2, 1, 3))
    x, cot = flip(tokens), flip(cotangent)
    if linked:
        shape = chip_grid(n_dp // 2) + (n_mp,)
        g, vectors, kept = forward(shape, micro, x, cot, domain_ids, domain_counts, weights, [norm.reshape(1, -1) for norm in norms])
    else:
        shards = jnp.stack(
            weights[:4] + tuple(w[:, i * SEG : (i + 1) * SEG] for w in weights[4:] for i in range(2))
        )
        g = lax.all_gather(lax.all_gather(shards, "dp", axis=1, tiled=True), "mp", axis=1)
        vectors = lax.all_gather(jnp.stack(norms), "dp", axis=1, tiled=True).astype(F32)
        vectors = jnp.pad(vectors, ((0, 4), (0, 0)))
        g, vectors, kept = forward(None, micro, x, cot, domain_ids, domain_counts, None, None, g, vectors)
    shape = shape if linked else None
    results = feed_back(shape, vectors, g, kept)
    dw_f, gres, gm, vec_f = results[:4]
    kept = {**kept, "gres": gres, "gm": gm}
    if linked:
        out, grad_down = results[4:]
        grad_tokens, *grads, vec = attn_back(shape, vectors, vec_f, g, dw_f, kept)
        grads.append(grad_down)
        core = lax.rem(lax.axis_index("dp"), 2)
        vec = lax.dynamic_slice(vec, (0, core * share), (4, share))
    else:
        dw_a, low_tokens, vec_a = attn_back(shape, vectors, vec_f, g, dw_f, kept)
        dw = jnp.concatenate((dw_a, dw_f[4:], dw_f[:4])).astype(F32)
        dw = lax.psum_scatter(lax.psum_scatter(dw, "mp", scatter_dimension=1), "dp", scatter_dimension=1, tiled=True)
        grads = [dw[0], dw[1], dw[2], dw[3]]
        grads += [jnp.concatenate((dw[a], dw[b]), axis=1) for a, b in (UPS, DOWNS)]
        vec = jnp.concatenate((jnp.sum(vec_a, axis=1), jnp.sum(vec_f, axis=1)))
        vec = lax.psum_scatter(lax.psum(vec, "mp"), "dp", scatter_dimension=1, tiled=True)
        out = lax.all_gather(kept["out"], "mp", axis=0, tiled=True)
        grad_tokens = lax.all_gather(low_tokens, "mp", axis=0, tiled=True)
    return (flip(out), flip(grad_tokens.astype(F32)), *grads, vec[0], vec[1], vec[2], vec[3])


def solution(mesh):
    rows, matrix, vector = P(None, "dp", None, None), P("dp", "mp"), P("dp")
    in_specs = (rows, rows, P(None, "dp"), P()) + (matrix,) * 6 + (vector,) * 4
    out_specs = (rows, rows) + (matrix,) * 6 + (vector,) * 4
    run = functools.partial(body, (mesh.shape["dp"], mesh.shape["mp"]))
    return jax.shard_map(run, mesh=mesh, in_specs=in_specs, out_specs=out_specs, check_vma=False)
```

profile of v0, /device:TPU:0, one launch (start us, length us, event | category | flops | bytes accessed | tf_op | source)
XLA Modules:
  0.0 256.5 jit_solution(14082766019148133227)
XLA Ops:
  0.6 96.4 %forward.1 = (bf16[8,2,4,2,2,64,512]{6,5,4,3,2,1,0:T(8,128)(2,1)}, f32[8,1024]{1,0:T(8,128)}, bf16[768,1024]{1,0:T(8,128)(2,1)}, bf16[768,1024]{1,0:T(8,128)(2,1...) custom-call(bf16[4,15,24,1024]{3,2,1,0:T(8,128)(2,1)} %bitcast.17, ...), custom_call_target="tpu_custom_call" | custom-call | tf_op jit(solution)/shard_map/forward/pallas_call | solution.py:1063
  97.1 54.6 %feed_back.1 = (bf16[5,2,4,2,2,64,512]{6,5,4,3,2,1,0:T(8,128)(2,1)}, f32[768,1024]{1,0:T(8,128)}, bf16[768,1024]{1,0:T(8,128)(2,1)}, f32[2,8,1024]{2,1,0:T(8,128...) custom-call(f32[8,1024]{1,0:T(8,128)} %get-tuple-element.43.vectors, ...), custom_call_target="tpu_custom_call" | custom-call | tf_op jit(solution)/shard_map/feed_back/pallas_call | solution.py:1122
  151.7 93.0 %attn_back.1 = (bf16[4,15,24,1024]{3,2,1,0:T(8,128)(2,1)}, f32[64,512]{1,0:T(8,128)}, f32[64,512]{1,0:T(8,128)}, f32[64,512]{1,0:T(8,128)}, f32[64,512]{1,0:T(8,...) custom-call(f32[8,1024]{1,0:T(8,128)} %get-tuple-element.43.vectors, f32[2,8,1024]{2,1,0:T(8,128)} %get-tuple-element.56.vec_f, ...), custom_call_target="tpu_custom_call" | custom-call | tf_op jit(solution)/shard_map/attn_back/pallas_call | solution.py:1155
  244.7 0.0 copy-start.7
  244.7 0.0 copy-start
  244.7 5.3 %convert_bitcast_fusion = f32[4,24,15,1024]{3,1,2,0:T(8,128)} fusion(bf16[4,15,24,1024]{3,2,1,0:T(8,128)(2,1)} %get-tuple-element.66), kind=kLoop, calls=%fused_computation | loop fusion | flops 1474560 | bytes 8847360 | tf_op jit(solution)/shard_map/transpose | solution.py:1181
  250.0 0.0 copy-done.7
  250.0 0.1 constant_dynamic-slice_fusion
  250.0 0.5 slice_bitcast_fusion
  250.6 0.0 copy-done
  250.6 0.0 copy-start.6
  250.6 0.0 copy-start.5
  250.6 0.0 copy-start.4
  250.6 0.0 copy-start.3
  250.6 0.0 copy-start.2
  250.6 0.0 copy-start.1
  250.6 1.6 copy.33
  252.2 0.0 copy-done.6
  252.2 0.7 copy.34
  252.9 0.0 copy-done.5
  252.9 0.7 copy.35
  253.5 0.0 copy-done.4
  253.5 0.7 copy.36
  254.2 0.0 copy-done.3
  254.2 0.7 copy.37
  254.9 0.0 copy-done.2
  254.9 0.7 copy.38
  255.6 0.0 copy-done.1
  255.6 0.7 copy.39
Async XLA Ops:
  244.7 5.3 %copy-start.7 = (f32[8,128]{1,0:T(8,128)S(1)}, f32[8,128]{1,0:T(8,128)}, u32[]{:S(2)}) copy-start(f32[8,128]{1,0:T(8,128)} %get-tuple-element.73) | copy-start | bytes 12292
  244.7 5.9 %copy-start = (bf16[4,15,24,1024]{3,2,1,0:T(8,128)(2,1)S(1)}, bf16[4,15,24,1024]{3,2,1,0:T(8,128)(2,1)}, u32[]{:S(2)}) copy-start(bf16[4,15,24,1024]{3,2,1,0:T(8,128)(2,1)} %get-tuple-element.55) | copy-start | bytes 8847364
  250.6 1.6 copy-start.6
  250.6 2.3 copy-start.5
  250.6 3.0 %copy-start.4 = (f32[64,512]{1,0:T(8,128)S(1)}, f32[64,512]{1,0:T(8,128)}, u32[]{:S(2)}) copy-start(f32[64,512]{1,0:T(8,128)} %get-tuple-element.94) | copy-start | bytes 393220
  250.6 3.6 %copy-start.3 = (f32[64,512]{1,0:T(8,128)S(1)}, f32[64,512]{1,0:T(8,128)}, u32[]{:S(2)}) copy-start(f32[64,512]{1,0:T(8,128)} %get-tuple-element.95) | copy-start | bytes 393220
  250.6 4.3 %copy-start.2 = (f32[64,1024]{1,0:T(8,128)S(1)}, f32[64,1024]{1,0:T(8,128)}, u32[]{:S(2)}) copy-start(f32[64,1024]{1,0:T(8,128)} %get-tuple-element.96) | copy-start | bytes 786436
  250.6 5.0 %copy-start.1 = (f32[64,1024]{1,0:T(8,128)S(1)}, f32[64,1024]{1,0:T(8,128)}, u32[]{:S(2)}) copy-start(f32[64,1024]{1,0:T(8,128)} %get-tuple-element.97) | copy-start | bytes 786436
where the time goes:
time: 261 us; the launch traced here: 256 us
  Pallas kernels  244 us (93%)
  local copies, waits for them, and re-layouts  6.26 us (2%)
  other arithmetic  5.27 us (2%)
    pallas_call x1, Pallas kernels, forward(): call(functools.partial(forward_kernel, shape, micro), (shape_of(full, BF)...  96.4 us
    pallas_call x1, Pallas kernels, attn_back(): call(functools.partial(attn_back_kernel, shape), tuple(outs), [IN_VMEM] *...  93 us
    pallas_call x1, Pallas kernels, feed_back(): call(functools.partial(feed_back_kernel, shape), tuple(outs), [IN_VMEM] +...  54.6 us
    unnamed x23, local copies, waits for them, and re-layouts  5.66 us
    transpose x1, other arithmetic, body(): flip = lambda array: jnp.transpose(array, (0, 2, 1, 3))  5.27 us

commit v1 on v0

--- a/solution.py
+++ b/solution.py
@@ -20,24 +20,24 @@
 Q, K, V, O, U0, U1, D0, D1 = range(8)
 UPS = (U0, U1)
 DOWNS = (D0, D1)
-ORDERS = ("zyx", "xyz", "zxy", "zyx", "zxy", "yxz", "zyx", "yxz")
-BACK_ORDERS = ("xzy", "xzy", "yxz", "zxy", "yzx", "xyz", "zxy", "xyz")
+ORDERS = ("zyx", "xyz", "zxy", "zyx", "zxy", "yxz", "zxy", "zyx")
+BACK_ORDERS = ("yxz", "xzy", "xzy", "xzy", "zxy", "yzx", "zxy", "xyz")
 
 FORWARD_PLAN = (
-    2, 1, 8, 4, 5, 6, 2, 8, 0, -1, 2, 4, 2, 0, 1, 3, 0, 4, 6, 3, 7, 8, 1, 5,
-    0, 2, 8, 4, 0, 3, 3, 1, 8, -1, 6, 6, 1, 5, -1, 7, 2, 4, 0, 3, 1, -1, -1, 5,
-    -1, -1, 7, -1, 3, 6, 5, -1, -1, 7, 4, -1, -1, 5, -1, 6, 7, -1, -1, 7, -1, -1, -1,
+    0, 8, 1, 2, 3, 8, 0, 5, 1, 2, -1, 5, 8, 4, 0, 0, 2, 3, 2, 6, 4, 8, 3, 1,
+    4, 3, 0, -1, 2, 8, 1, 4, -1, 1, 0, 3, 6, -1, 7, 2, 1, 4, 6, 5, -1, -1, -1, 6,
+    7, -1, 7, 3, 5, 7, -1, -1, 6, 4, -1, 7, 5, -1, 5, -1, -1, 6, -1, 7, -1, -1, -1,
 )
 FEED_PLAN = (
-    2, -1, 0, -1, -1, 1, 2, 0, 1, -1, 2, -1, 0, -1, -1, -1, 0, 1, -1, 2, -1, 0, 1, -1,
-    1, 0, -1, 1, -1, 0, 1,
+    2, -1, 0, -1, -1, 1, 0, 2, 2, 1, -1, -1, 0, -1, -1, -1, 0, 1, -1, 2, -1, 0, 1, -1,
+    1, -1, 0, 1, -1, 0, 1,
 )
 ATTN_PLAN = (
-    0, 2, -1, 1, -1, 1, 0, -1, -1, 2, -1, 3, -1, 1, -1, 5, 2, 3, -1, 5, 0, -1, -1, 2,
-    -1, 7, 4, 3, 6, 6, 1, 7, 4, 6, 5, 7, 0, 2, 1, 1, 7, 3, 3, 0, 4, 4, 6, 5,
-    2, 4, 0, 5, 1, 6, 4, 3, 5, 0, 4, 2, 6, 5, 3,
+    -1, 2, 1, 0, -1, 0, 2, 1, -1, -1, -1, -1, 3, 0, -1, 4, 3, 1, -1, 5, 4, 0, -1, 7,
+    1, 2, 7, 5, 1, -1, 2, 2, 8, 3, 4, -1, 4, 6, 8, 4, 6, 1, 5, 3, 6, 5, 2, 6,
+    3, 0, 5, 6, 3, 4, 0, 6, 5, 4, 0, 1, 3, 2, 5,
 )
-GRADS_FIRST = 3
+GRADS_FIRST = 1
 
 
 def nn(a, b):
@@ -730,7 +730,7 @@
         self.mover, self.source, self.ready = mover, source, ready
         y, (micro, patches) = place.at["y"], source.shape[:2]
         cut = patches // 2 + 1
-        self.spot = target.at[pl.ds(y * micro, micro)]
+        self.spots = [target.at[y * micro + part] for part in range(micro)]
         self.copies = []
         for part in range(micro):
             for piece in (pl.ds(0, cut), pl.ds(cut, patches - cut)):
@@ -746,13 +746,14 @@
                     )
                 )
 
-    def start(self):
-        self.ready()
-        self.copies[0].start()
-        self.mover.save(self.source, self.spot)
-
-    def steps(self):
-        return [self.start] + [copy.start for copy in self.copies[1:]]
+    def start(self, part):
+        if part == 0:
+            self.ready()
+        self.copies[2 * part].start()
+        self.mover.save(self.source.at[part], self.spots[part])
+
+    def steps(self, part):
+        return [functools.partial(self.start, part), self.copies[2 * part + 1].start]
 
     def wait(self):
         for copy in self.copies:
@@ -766,6 +767,10 @@
         dw_out, gres_out, gm_out, vec, refs = refs[:4] + (refs[4:],)
     cot, weight, active, slope, nrm2, res, g, dw, gl, glt, gh, n2t, gn2, gres, mix, gm, sems = refs[:17]
     mover = Mover(sems)
+    if shape:
+        half_out, hands, send, recv, ysem = refs[17:22]
+        boxes = list(refs[22:])
+        side = mover.start(out_in, half_out)
     loads = {"glt": mover.start(glt_in, glt), ("active", 0): mover.start(active_in.at[0], active.at[0])}
     loads["gl"] = mover.start(gl_in, gl)
     for which in range(2):
@@ -783,9 +788,6 @@
     loads["weight"] = mover.start(weight_in, weight)
     comm = {}
     if shape:
-        half_out, hands, send, recv, ysem = refs[17:22]
-        boxes = list(refs[22:])
-        side = mover.start(out_in, half_out)
         place = Place(shape)
         place.barrier("zxy")
         runs = []
@@ -797,7 +799,7 @@
             open_inbox(run, place.count, "yzx", order, dw.shape[-2:], boxes)
             runs.append(run)
         swap = Swap(place, mover, ysem, side.wait, half_out, pair)
-        comm = {0: runs[0].steps(), 1: runs[1].steps(), 2: swap.steps()}
+        comm = {0: runs[0].steps(), 1: runs[1].steps(), 2: swap.steps(0) + swap.steps(1)}
 
     def down_grad(which):
         if which == 0:
@@ -900,15 +902,23 @@
     else:
         dw_out, out, vec, refs = refs[0], refs[1], refs[2], refs[3:]
     here = dict(zip(BACK_IN, refs[:8]))
-    g, dw, gal, gq, gk, gv, raw, sems = refs[8:16]
+    g, dw, gal, pulls, raw, sems = refs[8:14]
     mover = Mover(sems)
     loads, comm = {}, {}
     if shape:
-        held, tiles, hands, vec_hand, ybox, vec, send, recv, ysem = refs[16:25]
-        boxes = list(refs[25:])
-        for spot, part in enumerate(KEPT_GRADS):
-            loads["dw", spot] = mover.start(dw_in.at[part], held.at[spot])
-    for name in BACK_IN:
+        held, tiles, hands, vec_hand, ybox, vec, send, recv, ysem = refs[14:23]
+        boxes = list(refs[23:])
+
+    def fetch_held(*spots):
+        for spot in spots:
+            if shape:
+                loads["dw", spot] = mover.start(dw_in.at[KEPT_GRADS[spot]], held.at[spot])
+
+    fetch_held(0)
+    for name in BACK_IN[:5]:
+        loads[name] = mover.start(given[name], here[name])
+    fetch_held(1, 2)
+    for name in BACK_IN[5:]:
         loads[name] = mover.start(given[name], here[name])
     for seg in (Q, K, V):
         loads[seg] = mover.start(g_in.at[seg], g.at[seg])
@@ -929,35 +939,39 @@
         runs.append(run)
         swap = Swap(place, mover, ysem, lambda: None, raw, pair)
         comm = {spot: run.steps() for spot, run in enumerate(runs)}
-        comm[7] = swap.steps()
+        comm[7], comm[8] = swap.steps(0), swap.steps(1)
         for spot in range(3):
             comm[spot][0] = lambda spot=spot: (loads["dw", spot].wait(), runs[spot].start())
 
     third = gal.shape[0] // TILE // 3
+    micro = raw.shape[0]
+    share = gal.shape[0] // micro
 
     def ready():
-        for name in BACK_IN[:6]:
+        for name in BACK_IN[:5]:
             loads[name].wait()
+        vec[...] = jnp.zeros_like(vec)
 
     def mixing(part):
-        attend_back(q, k, v, probs, gm, gq, gk, gv, part * third, third)
-
-    def head_grad(seg, grad):
-        weight_grad(nrmt, lambda m: grad[:, half(m)], dw, seg)
-        if not shape:
-            mover.save(dw.at[seg], dw_out.at[seg])
-
-    def norm_grad(seg, grad):
-        if seg == Q:
-            gn[...] = jnp.zeros_like(gn)
-        loads[seg].wait()
-        back_through(lambda m: grad[:, half(m)], g, seg, gn)
-
-    def last():
-        loads["gres"].wait()
-        loads["x"].wait()
+        attend_back(q, k, v, probs, gm, pulls.at[0], pulls.at[1], pulls.at[2], part * third, third)
+
+    def head_grad(seg):
+        weight_grad(nrmt, lambda m: pulls[seg, :, half(m)], dw, seg)
+
+    def token_grad(part):
+        rows_of = pl.ds(part * share, share)
+        gn[rows_of, :] = jnp.zeros((share, gn.shape[1]), F32)
+        if part == 0:
+            for name in (Q, K, V, "gres", "x"):
+                loads[name].wait()
+
+        def one(index, carry):
+            seg, m = lax.div(index, 2), lax.rem(index, 2)
+            gn[rows_of, :] += nt(pulls[seg, rows_of, half(m)], flat(g[seg, m]))
+            return carry
+
+        lax.fori_loop(0, 6, one, 0)
         gain = vectors[0:1, :]
-        vec[...] = jnp.zeros_like(vec)
 
         def block(rows, _):
             grad = gn[rows, :]
@@ -966,19 +980,28 @@
             vec[1] += fold_rows(grad)
             gal[rows, :] = (gres[rows, :] + pulled).astype(BF)
 
-        row_loop(gal.shape[0], block)
-        from_rows(gal, raw)
+        row_loop(share, block, part * share // TILE)
+        patches, series, width = raw.shape[1:]
+        turned = nn(gather_rows(patches, series), gal[rows_of, :]).astype(raw.dtype)
+        raw[part] = turned.reshape(patches, series, width)
+
+    def spread_vectors():
         if shape:
             vector_tiles(tiles, vec, vec_f)
-        else:
-            mover.save(raw, out)
-
-    heads = ((Q, gq), (K, gk), (V, gv))
-    pieces = [ready, (3, mixing)]
-    pieces += [functools.partial(head_grad, *pair_of) for pair_of in heads[:GRADS_FIRST]]
-    pieces += [functools.partial(norm_grad, *pair_of) for pair_of in heads] + [last]
-    pieces += [functools.partial(head_grad, *pair_of) for pair_of in heads[GRADS_FIRST:]]
+
+    def before_heads():
+        loads["nrmt"].wait()
+
+    pieces = [ready, (3, mixing), before_heads]
+    parts = [functools.partial(token_grad, part) for part in range(micro)]
+    heads = [(3, head_grad)]
+    pieces += heads + parts if GRADS_FIRST else parts + heads
+    pieces.insert(len(pieces) - (0 if GRADS_FIRST else 1), spread_vectors)
     play(ATTN_PLAN, comm, pieces)
+    if not shape:
+        mover.save(raw, out)
+        for seg in (Q, K, V):
+            mover.save(dw.at[seg], dw_out.at[seg])
     if shape:
         here_tile = tiles.at[place.at["z"], place.at["x"]]
         copy = pltpu.make_async_remote_copy(
@@ -1135,7 +1158,7 @@
     width = low.shape[1]
     part = shape_of((3,) + g.shape[1:], BF)
     scratch = [vmem(kept[name]) for name in BACK_IN]
-    scratch += [vmem(part), vmem(part), vmem(low), vmem(low), vmem(low), vmem(low), vmem(raw), DMA((32,))]
+    scratch += [vmem(part), vmem(part), vmem(low), pltpu.VMEM((3,) + low.shape, BF), vmem(raw), DMA((32,))]
     vec = shape_of((2, 8, width), F32)
     if shape:
         nz, nx, ny = shape

time: 261 us -> 235 us (0.900); the launches traced: 256 us -> 235 us
  Pallas kernels: 244 us -> 222 us
    pallas_call x1, Pallas kernels: 93 us -> 80.8 us  [attn_back(): call(functools.partial(attn_back_kernel, shape), tuple(outs), [IN_VMEM] *...]
    pallas_call x1, Pallas kernels: 54.6 us -> 47.3 us  [feed_back(): call(functools.partial(feed_back_kernel, shape), tuple(outs), [IN_VMEM] +...]
where the time goes in v1:
time: 235 us
  Pallas kernels  222 us (94%)
  local copies, waits for them, and re-layouts  6.26 us (3%)
  other arithmetic  5.27 us (2%)
    pallas_call x1, Pallas kernels, forward(): call(functools.partial(forward_kernel, shape, micro), (shape_of(full, BF)...  94.2 us
    pallas_call x1, Pallas kernels, attn_back(): call(functools.partial(attn_back_kernel, shape), tuple(outs), [IN_VMEM] *...  80.8 us
    pallas_call x1, Pallas kernels, feed_back(): call(functools.partial(feed_back_kernel, shape), tuple(outs), [IN_VMEM] +...  47.3 us
    unnamed x23, local copies, waits for them, and re-layouts  5.66 us
    transpose x1, other arithmetic, body(): flip = lambda array: jnp.transpose(array, (0, 2, 1, 3))  5.27 us

profile of v1, /device:TPU:0, one launch (start us, length us, event | category | flops | bytes accessed | tf_op | source)
XLA Modules:
  0.0 234.5 jit_solution(10953604146674641044)
XLA Ops:
  0.6 94.2 %forward.1 = (bf16[8,2,4,2,2,64,512]{6,5,4,3,2,1,0:T(8,128)(2,1)}, f32[8,1024]{1,0:T(8,128)}, bf16[768,1024]{1,0:T(8,128)(2,1)}, bf16[768,1024]{1,0:T(8,128)(2,1...) custom-call(bf16[4,15,24,1024]{3,2,1,0:T(8,128)(2,1)} %bitcast.17, ...), custom_call_target="tpu_custom_call" | custom-call | tf_op jit(solution)/shard_map/forward/pallas_call | solution.py:1086
  94.9 47.3 %feed_back.1 = (bf16[5,2,4,2,2,64,512]{6,5,4,3,2,1,0:T(8,128)(2,1)}, f32[768,1024]{1,0:T(8,128)}, bf16[768,1024]{1,0:T(8,128)(2,1)}, f32[2,8,1024]{2,1,0:T(8,128...) custom-call(f32[8,1024]{1,0:T(8,128)} %get-tuple-element.43.vectors, ...), custom_call_target="tpu_custom_call" | custom-call | tf_op jit(solution)/shard_map/feed_back/pallas_call | solution.py:1145
  142.1 80.8 %attn_back.1 = (bf16[4,15,24,1024]{3,2,1,0:T(8,128)(2,1)}, f32[64,512]{1,0:T(8,128)}, f32[64,512]{1,0:T(8,128)}, f32[64,512]{1,0:T(8,128)}, f32[64,512]{1,0:T(8,...) custom-call(f32[8,1024]{1,0:T(8,128)} %get-tuple-element.43.vectors, f32[2,8,1024]{2,1,0:T(8,128)} %get-tuple-element.56.vec_f, ...), custom_call_target="tpu_custom_call" | custom-call | tf_op jit(solution)/shard_map/attn_back/pallas_call | solution.py:1178
  222.9 0.0 copy-start.7
  222.9 0.0 copy-start
  222.9 5.3 %convert_bitcast_fusion = f32[4,24,15,1024]{3,1,2,0:T(8,128)} fusion(bf16[4,15,24,1024]{3,2,1,0:T(8,128)(2,1)} %get-tuple-element.66), kind=kLoop, calls=%fused_computation | loop fusion | flops 1474560 | bytes 8847360 | tf_op jit(solution)/shard_map/transpose | solution.py:1204
  228.2 0.0 copy-done.7
  228.2 0.1 constant_dynamic-slice_fusion
  228.3 0.5 slice_bitcast_fusion
  228.8 0.0 copy-done
  228.8 0.0 copy-start.6
  228.8 0.0 copy-start.5
  228.8 0.0 copy-start.4
  228.8 0.0 copy-start.3
  228.8 0.0 copy-start.2
  228.8 0.0 copy-start.1
  228.9 1.6 copy.33
  230.5 0.0 copy-done.6
  230.5 0.7 copy.34
  231.1 0.0 copy-done.5
  231.1 0.7 copy.35
  231.8 0.0 copy-done.4
  231.8 0.7 copy.36
  232.4 0.0 copy-done.3
  232.4 0.7 copy.37
  233.1 0.0 copy-done.2
  233.1 0.7 copy.38
  233.8 0.0 copy-done.1
  233.8 0.7 copy.39
Async XLA Ops:
  222.9 5.3 %copy-start.7 = (f32[8,128]{1,0:T(8,128)S(1)}, f32[8,128]{1,0:T(8,128)}, u32[]{:S(2)}) copy-start(f32[8,128]{1,0:T(8,128)} %get-tuple-element.73) | copy-start | bytes 12292
  222.9 5.9 %copy-start = (bf16[4,15,24,1024]{3,2,1,0:T(8,128)(2,1)S(1)}, bf16[4,15,24,1024]{3,2,1,0:T(8,128)(2,1)}, u32[]{:S(2)}) copy-start(bf16[4,15,24,1024]{3,2,1,0:T(8,128)(2,1)} %get-tuple-element.55) | copy-start | bytes 8847364
  228.8 1.6 copy-start.6
  228.8 2.3 copy-start.5
  228.8 3.0 %copy-start.4 = (f32[64,512]{1,0:T(8,128)S(1)}, f32[64,512]{1,0:T(8,128)}, u32[]{:S(2)}) copy-start(f32[64,512]{1,0:T(8,128)} %get-tuple-element.94) | copy-start | bytes 393220
  228.8 3.6 %copy-start.3 = (f32[64,512]{1,0:T(8,128)S(1)}, f32[64,512]{1,0:T(8,128)}, u32[]{:S(2)}) copy-start(f32[64,512]{1,0:T(8,128)} %get-tuple-element.95) | copy-start | bytes 393220
  228.8 4.3 %copy-start.2 = (f32[64,1024]{1,0:T(8,128)S(1)}, f32[64,1024]{1,0:T(8,128)}, u32[]{:S(2)}) copy-start(f32[64,1024]{1,0:T(8,128)} %get-tuple-element.96) | copy-start | bytes 786436
  228.8 5.0 %copy-start.1 = (f32[64,1024]{1,0:T(8,128)S(1)}, f32[64,1024]{1,0:T(8,128)}, u32[]{:S(2)}) copy-start(f32[64,1024]{1,0:T(8,128)} %get-tuple-element.97) | copy-start | bytes 786436

commit v2 on v1

--- a/solution.py
+++ b/solution.py
@@ -20,22 +20,22 @@
 Q, K, V, O, U0, U1, D0, D1 = range(8)
 UPS = (U0, U1)
 DOWNS = (D0, D1)
-ORDERS = ("zyx", "xyz", "zxy", "zyx", "zxy", "yxz", "zxy", "zyx")
-BACK_ORDERS = ("yxz", "xzy", "xzy", "xzy", "zxy", "yzx", "zxy", "xyz")
+ORDERS = ("zyx", "zxy", "zxy", "yzx", "xyz", "zxy", "zyx", "xyz")
+BACK_ORDERS = ("yxz", "xzy", "xzy", "zxy", "xzy", "yxz", "zxy", "xyz")
 
 FORWARD_PLAN = (
-    0, 8, 1, 2, 3, 8, 0, 5, 1, 2, -1, 5, 8, 4, 0, 0, 2, 3, 2, 6, 4, 8, 3, 1,
-    4, 3, 0, -1, 2, 8, 1, 4, -1, 1, 0, 3, 6, -1, 7, 2, 1, 4, 6, 5, -1, -1, -1, 6,
-    7, -1, 7, 3, 5, 7, -1, -1, 6, 4, -1, 7, 5, -1, 5, -1, -1, 6, -1, 7, -1, -1, -1,
+    2, 1, 8, 4, 0, 3, 4, 2, 7, 8, -1, 0, 2, 7, 8, 1, 2, 0, 6, 0, 1, 5, 3, 1,
+    2, 8, 5, 4, 0, 5, 8, 6, -1, 6, 3, 1, 5, 3, 3, 0, 4, -1, 2, 6, -1, 4, 1, 5,
+    7, -1, -1, 6, -1, 4, 3, -1, 7, -1, -1, -1, -1, 5, 7, -1, -1, 6, -1, 7, -1, -1, -1,
 )
 FEED_PLAN = (
-    2, -1, 0, -1, -1, 1, 0, 2, 2, 1, -1, -1, 0, -1, -1, -1, 0, 1, -1, 2, -1, 0, 1, -1,
+    2, -1, 0, -1, -1, 1, 0, 2, 2, 1, -1, -1, -1, 0, -1, -1, 1, 2, 0, -1, -1, -1, 1, 0,
     1, -1, 0, 1, -1, 0, 1,
 )
 ATTN_PLAN = (
-    -1, 2, 1, 0, -1, 0, 2, 1, -1, -1, -1, -1, 3, 0, -1, 4, 3, 1, -1, 5, 4, 0, -1, 7,
-    1, 2, 7, 5, 1, -1, 2, 2, 8, 3, 4, -1, 4, 6, 8, 4, 6, 1, 5, 3, 6, 5, 2, 6,
-    3, 0, 5, 6, 3, 4, 0, 6, 5, 4, 0, 1, 3, 2, 5,
+    0, 1, -1, 1, 0, -1, 2, -1, -1, -1, -1, 3, 2, -1, 4, 3, -1, 2, 4, 0, 5, -1, 7, 0,
+    5, 1, 0, 7, 3, 2, 4, -1, 8, -1, 0, 4, 5, 5, 8, 6, 6, 1, 4, 6, 5, 2, 6, 4,
+    3, 1, 5, 6, 3, 1, 2, 6, 3, 5, 1, 4, 0, 3, 2,
 )
 GRADS_FIRST = 1
 
@@ -73,9 +73,9 @@
 
 
 def score_mask():
-    row = lax.broadcasted_iota(jnp.int32, (TILE, TILE), 0)
-    col = lax.broadcasted_iota(jnp.int32, (TILE, TILE), 1)
-    return (row // PAD == col // PAD) & (col <= row)
+    key = lax.broadcasted_iota(jnp.int32, (TILE, TILE), 0)
+    query = lax.broadcasted_iota(jnp.int32, (TILE, TILE), 1)
+    return (query // PAD == key // PAD) & (key <= query)
 
 
 def row_loop(rows, body, first=0):
@@ -145,36 +145,41 @@
 def attend(queries, keys, values, probs, mixture, first, count):
     mask = score_mask()
     scale = HD ** (-0.5)
-
-    def group(rows, index):
-        for head in range(queries.shape[1] // HD):
-            cols = slice(head * HD, (head + 1) * HD)
-            scores = nt(queries[rows, cols], keys[rows, cols]) * scale
-            scores = jnp.where(mask, scores, -1e30)
-            powers = jnp.exp(scores - jnp.max(scores, axis=-1, keepdims=True))
-            share = powers * (1.0 / jnp.sum(powers, axis=-1, keepdims=True))
+    columns = [slice(at, at + HD) for at in range(0, queries.shape[1], HD)]
+
+    def group(rows, _):
+        scores = [nt(keys[rows, cols], queries[rows, cols]) * scale for cols in columns]
+        scores = [jnp.where(mask, score, -1e30) for score in scores]
+        peaks = [jnp.max(score, axis=0, keepdims=True) for score in scores]
+        powers = [jnp.exp(score - peak) for score, peak in zip(scores, peaks)]
+        inverses = [1.0 / jnp.sum(power, axis=0, keepdims=True) for power in powers]
+        shares = [power * inverse for power, inverse in zip(powers, inverses)]
+        for cols, share in zip(columns, shares):
             probs[rows, cols] = share
-            mixture[rows, cols] = nn(share.astype(BF), values[rows, cols]).astype(BF)
+        mixed = [nn(share.astype(BF).T, values[rows, cols]) for share, cols in zip(shares, columns)]
+        for cols, part in zip(columns, mixed):
+            mixture[rows, cols] = part.astype(BF)
 
     row_loop(count * TILE, group, first)
 
 
 def attend_back(queries, keys, values, probs, grad_mix, grad_q, grad_k, grad_v, first, count):
     scale = HD ** (-0.5)
-
-    def group(rows, index):
-        for head in range(queries.shape[1] // HD):
-            cols = slice(head * HD, (head + 1) * HD)
-            share = probs[rows, cols]
-            grad = grad_mix[rows, cols]
-            grad_share = nt(grad, values[rows, cols])
-            grad_v[rows, cols] = nn(share.T.astype(BF), grad).astype(BF)
-            inner = jnp.sum(grad_share * share, axis=-1, keepdims=True)
-            grad_scores = share * (grad_share - inner)
-            low = grad_scores.astype(BF)
-            grad_q[rows, cols] = (nn(low, keys[rows, cols]) * scale).astype(BF)
-            turned = grad_scores.T.astype(BF)
-            grad_k[rows, cols] = (nn(turned, queries[rows, cols]) * scale).astype(BF)
+    columns = [slice(at, at + HD) for at in range(0, queries.shape[1], HD)]
+
+    def group(rows, _):
+        shares = [probs[rows, cols] for cols in columns]
+        grads = [grad_mix[rows, cols] for cols in columns]
+        pulls = [nt(values[rows, cols], grad) for cols, grad in zip(columns, grads)]
+        back_v = [nn(share.astype(BF), grad) for share, grad in zip(shares, grads)]
+        inner = [jnp.sum(pull * share, axis=0, keepdims=True) for pull, share in zip(pulls, shares)]
+        lows = [(share * (pull - mean)).astype(BF) for share, pull, mean in zip(shares, pulls, inner)]
+        back_k = [nn(low, queries[rows, cols]) * scale for low, cols in zip(lows, columns)]
+        back_q = [nn(low.T, keys[rows, cols]) * scale for low, cols in zip(lows, columns)]
+        for cols, one, two, three in zip(columns, back_q, back_k, back_v):
+            grad_q[rows, cols] = one.astype(BF)
+            grad_k[rows, cols] = two.astype(BF)
+            grad_v[rows, cols] = three.astype(BF)
 
     row_loop(count * TILE, group, first)
 

time: 235 us -> 217 us (0.923)
  Pallas kernels: 222 us -> 205 us
    pallas_call x1, Pallas kernels: 94.2 us -> 83 us  [forward(): call(functools.partial(forward_kernel, shape, micro), (shape_of(full, BF)...]
    pallas_call x1, Pallas kernels: 80.8 us -> 73.5 us  [attn_back(): call(functools.partial(attn_back_kernel, shape), tuple(outs), [IN_VMEM] *...]
where the time goes in v2:
time: 217 us
  Pallas kernels  205 us (94%)
  local copies, waits for them, and re-layouts  6.26 us (3%)
  other arithmetic  5.27 us (2%)
    pallas_call x1, Pallas kernels, forward(): call(functools.partial(forward_kernel, shape, micro), (shape_of(full, BF)...  83 us
    pallas_call x1, Pallas kernels, attn_back(): call(functools.partial(attn_back_kernel, shape), tuple(outs), [IN_VMEM] *...  73.5 us
    pallas_call x1, Pallas kernels, feed_back(): call(functools.partial(feed_back_kernel, shape), tuple(outs), [IN_VMEM] +...  48.4 us
    unnamed x23, local copies, waits for them, and re-layouts  5.66 us
    transpose x1, other arithmetic, body(): flip = lambda array: jnp.transpose(array, (0, 2, 1, 3))  5.27 us

profile of v2, /device:TPU:0, one launch (start us, length us, event | category | flops | bytes accessed | tf_op | source)
XLA Modules:
  0.0 217.1 jit_solution(91592939704605082)
XLA Ops:
  0.6 83.0 %forward.1 = (bf16[8,2,4,2,2,64,512]{6,5,4,3,2,1,0:T(8,128)(2,1)}, f32[8,1024]{1,0:T(8,128)}, bf16[768,1024]{1,0:T(8,128)(2,1)}, bf16[768,1024]{1,0:T(8,128)(2,1...) custom-call(bf16[4,15,24,1024]{3,2,1,0:T(8,128)(2,1)} %bitcast.17, ...), custom_call_target="tpu_custom_call" | custom-call | tf_op jit(solution)/shard_map/forward/pallas_call | solution.py:1091
  83.6 48.4 %feed_back.1 = (bf16[5,2,4,2,2,64,512]{6,5,4,3,2,1,0:T(8,128)(2,1)}, f32[768,1024]{1,0:T(8,128)}, bf16[768,1024]{1,0:T(8,128)(2,1)}, f32[2,8,1024]{2,1,0:T(8,128...) custom-call(f32[8,1024]{1,0:T(8,128)} %get-tuple-element.43.vectors, ...), custom_call_target="tpu_custom_call" | custom-call | tf_op jit(solution)/shard_map/feed_back/pallas_call | solution.py:1150
  132.0 73.5 %attn_back.1 = (bf16[4,15,24,1024]{3,2,1,0:T(8,128)(2,1)}, f32[64,512]{1,0:T(8,128)}, f32[64,512]{1,0:T(8,128)}, f32[64,512]{1,0:T(8,128)}, f32[64,512]{1,0:T(8,...) custom-call(f32[8,1024]{1,0:T(8,128)} %get-tuple-element.43.vectors, f32[2,8,1024]{2,1,0:T(8,128)} %get-tuple-element.56.vec_f, ...), custom_call_target="tpu_custom_call" | custom-call | tf_op jit(solution)/shard_map/attn_back/pallas_call | solution.py:1183
  205.5 0.0 copy-start.7
  205.5 0.0 copy-start
  205.5 5.3 %convert_bitcast_fusion = f32[4,24,15,1024]{3,1,2,0:T(8,128)} fusion(bf16[4,15,24,1024]{3,2,1,0:T(8,128)(2,1)} %get-tuple-element.66), kind=kLoop, calls=%fused_computation | loop fusion | flops 1474560 | bytes 8847360 | tf_op jit(solution)/shard_map/transpose | solution.py:1209
  210.8 0.0 copy-done.7
  210.8 0.1 constant_dynamic-slice_fusion
  210.9 0.5 slice_bitcast_fusion
  211.4 0.0 copy-done
  211.4 0.0 copy-start.6
  211.4 0.0 copy-start.5
  211.4 0.0 copy-start.4
  211.4 0.0 copy-start.3
  211.4 0.0 copy-start.2
  211.4 0.0 copy-start.1
  211.4 1.6 copy.33
  213.0 0.0 copy-done.6
  213.0 0.7 copy.34
  213.7 0.0 copy-done.5
  213.7 0.7 copy.35
  214.4 0.0 copy-done.4
  214.4 0.7 copy.36
  215.0 0.0 copy-done.3
  215.0 0.7 copy.37
  215.7 0.0 copy-done.2
  215.7 0.7 copy.38
  216.4 0.0 copy-done.1
  216.4 0.7 copy.39
Async XLA Ops:
  205.5 5.3 %copy-start.7 = (f32[8,128]{1,0:T(8,128)S(1)}, f32[8,128]{1,0:T(8,128)}, u32[]{:S(2)}) copy-start(f32[8,128]{1,0:T(8,128)} %get-tuple-element.73) | copy-start | bytes 12292
  205.5 5.9 %copy-start = (bf16[4,15,24,1024]{3,2,1,0:T(8,128)(2,1)S(1)}, bf16[4,15,24,1024]{3,2,1,0:T(8,128)(2,1)}, u32[]{:S(2)}) copy-start(bf16[4,15,24,1024]{3,2,1,0:T(8,128)(2,1)} %get-tuple-element.55) | copy-start | bytes 8847364
  211.4 1.6 copy-start.6
  211.4 2.3 %copy-start.5 = (f32[64,512]{1,0:T(8,128)S(1)}, f32[64,512]{1,0:T(8,128)}, u32[]{:S(2)}) copy-start(f32[64,512]{1,0:T(8,128)} %get-tuple-element.93) | copy-start | bytes 393220
  211.4 3.0 %copy-start.4 = (f32[64,512]{1,0:T(8,128)S(1)}, f32[64,512]{1,0:T(8,128)}, u32[]{:S(2)}) copy-start(f32[64,512]{1,0:T(8,128)} %get-tuple-element.94) | copy-start | bytes 393220
  211.4 3.6 %copy-start.3 = (f32[64,512]{1,0:T(8,128)S(1)}, f32[64,512]{1,0:T(8,128)}, u32[]{:S(2)}) copy-start(f32[64,512]{1,0:T(8,128)} %get-tuple-element.95) | copy-start | bytes 393220
  211.4 4.3 %copy-start.2 = (f32[64,1024]{1,0:T(8,128)S(1)}, f32[64,1024]{1,0:T(8,128)}, u32[]{:S(2)}) copy-start(f32[64,1024]{1,0:T(8,128)} %get-tuple-element.96) | copy-start | bytes 786436
  211.4 5.0 %copy-start.1 = (f32[64,1024]{1,0:T(8,128)S(1)}, f32[64,1024]{1,0:T(8,128)}, u32[]{:S(2)}) copy-start(f32[64,1024]{1,0:T(8,128)} %get-tuple-element.97) | copy-start | bytes 786436

commit v3 on v2

--- a/solution.py
+++ b/solution.py
@@ -20,17 +20,20 @@
 Q, K, V, O, U0, U1, D0, D1 = range(8)
 UPS = (U0, U1)
 DOWNS = (D0, D1)
-ORDERS = ("zyx", "zxy", "zxy", "yzx", "xyz", "zxy", "zyx", "xyz")
-BACK_ORDERS = ("yxz", "xzy", "xzy", "zxy", "xzy", "yxz", "zxy", "xyz")
+ORDERS = ("zxy", "zxy", "zyx", "zyx", "zxy", "zyx", "yzx", "zxy", "yxz", "zxy", "zyx", "yxz", "xzy", "zxy", "xyz", "yzx")
+BACK_ORDERS = ("yxz", "xzy", "xzy", "zxy", "xzy", "yxz")
+FEED_ORDERS = ("xzy", "zxy", "zxy", "xzy")
 
 FORWARD_PLAN = (
-    2, 1, 8, 4, 0, 3, 4, 2, 7, 8, -1, 0, 2, 7, 8, 1, 2, 0, 6, 0, 1, 5, 3, 1,
-    2, 8, 5, 4, 0, 5, 8, 6, -1, 6, 3, 1, 5, 3, 3, 0, 4, -1, 2, 6, -1, 4, 1, 5,
-    7, -1, -1, 6, -1, 4, 3, -1, 7, -1, -1, -1, -1, 5, 7, -1, -1, 6, -1, 7, -1, -1, -1,
+    3, 14, 7, 6, 5, 11, -1, 8, 15, 3, 7, 14, 11, 0, 10, 8, 12, 3, 3, 7, 5, 7, 0, 5,
+    0, 16, 4, 5, 1, 9, 0, 13, 16, 3, 7, 4, 1, 16, 16, 2, 6, 0, 1, 4, 13, 2, 13, 10,
+    1, 9, 4, 2, 15, 9, 16, 12, 6, 2, 1, 5, 7, 8, -1, -1, 3, 12, 2, 10, 6, 15, 4, 11,
+    0, 12, 5, 10, 9, 1, 8, 6, 13, -1, 2, 12, 4, 9, 11, -1, 14, -1, 10, -1, 6, 8, 15, -1,
+    12, -1, 11, 14, 13, -1, 15, 8, 9, -1, 11, 10, -1, -1, 14, -1, 13, -1, 15, 14, -1, -1, -1,
 )
 FEED_PLAN = (
-    2, -1, 0, -1, -1, 1, 0, 2, 2, 1, -1, -1, -1, 0, -1, -1, 1, 2, 0, -1, -1, -1, 1, 0,
-    1, -1, 0, 1, -1, 0, 1,
+    4, -1, 1, -1, 1, 0, -1, 3, 4, 0, 4, 1, 2, -1, 2, 3, -1, 1, -1, 0, 2, -1, 1, 0,
+    -1, 3, 1, 4, 2, -1, 3, 1, -1, 0, 2, 3, -1, 0, -1, 2, 3, -1, 0, 2, 3,
 )
 ATTN_PLAN = (
     0, 1, -1, 1, 0, -1, 2, -1, -1, -1, -1, 3, 2, -1, 4, 3, -1, 2, 4, 0, 5, -1, 7, 0,
@@ -503,7 +506,9 @@
         elif callable(pieces[0]):
             pieces.pop(0)()
         else:
-            count, piece = pieces.pop(0)
+            count, piece, before, after = pieces.pop(0)
+            if before:
+                before()
             between = [[] for _ in range(count - 1)]
             for spot in range(count - 1):
                 while plan[0] >= 0:
@@ -525,6 +530,8 @@
                 return carry
 
             lax.fori_loop(0, count, once, 0)
+            if after:
+                after()
     assert not pieces and not any(comm.values())
 
 
@@ -611,17 +618,30 @@
         fill_tile(place, tiles, norms)
         place.barrier("zxy")
         pick = lambda seg: tuple(sem.at[seg] for sem in (send, recv, pass_send, pass_recv))
-        runs = [Gather(place, g.at[seg], "yzx", ORDERS[seg], pick(seg)) for seg in range(8)]
-        runs.append(Gather(place, tiles, "zx", "zx", pick(8)))
-        comm = {seg: run.steps() for seg, run in enumerate(runs)}
-        for seg in range(8):
-            comm[seg][0] = lambda seg=seg: (mine[seg].wait(), runs[seg].start())
+        runs, cut = [], len(ORDERS) // 8
+        for spot, order in enumerate(ORDERS):
+            columns = pl.ds(spot % cut * (SEG // cut), SEG // cut)
+            runs.append(Gather(place, g.at[spot // cut, :, :, :, :, :, columns], "yzx", order, pick(spot)))
+        runs.append(Gather(place, tiles, "zx", "zx", pick(len(ORDERS))))
+        comm = {spot: run.steps() for spot, run in enumerate(runs)}
+        waiting = list(mine)
+
+        def begin(spot):
+            if waiting[spot // cut] is not None:
+                waiting[spot // cut].wait()
+                waiting[spot // cut] = None
+            runs[spot].start()
+
+        for spot in range(len(ORDERS)):
+            comm[spot][0] = functools.partial(begin, spot)
 
         def have(seg):
-            runs[seg].finish()
             if seg < 8:
+                for run in runs[seg * cut : (seg + 1) * cut]:
+                    run.finish()
                 mover.save(g.at[seg], g_out.at[seg])
             else:
+                runs[-1].finish()
                 read_vectors(vectors, tiles)
 
     else:
@@ -685,11 +705,11 @@
         keep("nrm2")
 
     def up(which, m):
-        if m == 0:
-            have(UPS[which])
         feed_up(nrm2, g, which, m, active, slope)
-        mover.save(active.at[which, m], saved["active"].at[which, m])
-        mover.save(slope.at[which, m], saved["slope"].at[which, m])
+
+    def keep_up(which):
+        mover.save(active.at[which], saved["active"].at[which])
+        mover.save(slope.at[which], saved["slope"].at[which])
 
     def down(which):
         have(DOWNS[which])
@@ -704,8 +724,10 @@
 
     pieces = [spread, weigh, norm_one]
     pieces += [functools.partial(head_part, *args) for args in ((Q, q, "q"), (K, k, "k"), (V, v, "v"))]
-    pieces += [(3, mixing), project_out, norm_two]
-    pieces += [functools.partial(up, which, m) for which in range(2) for m in range(2)]
+    pieces += [(3, mixing, None, None), project_out, norm_two]
+    for which in range(2):
+        before, after = functools.partial(have, UPS[which]), functools.partial(keep_up, which)
+        pieces.append((2, functools.partial(up, which), before, after))
     pieces += [functools.partial(down, which) for which in range(2)] + [last]
     play(FORWARD_PLAN, comm, pieces)
     if shape:
@@ -796,15 +818,16 @@
         place = Place(shape)
         place.barrier("zxy")
         runs = []
-        for which in range(2):
-            order = BACK_ORDERS[DOWNS[which]]
-            run = Scatter(
-                place, dw.at[2 + which], "yzx", order, {}, hands.at[which], (send.at[which], recv.at[which])
-            )
-            open_inbox(run, place.count, "yzx", order, dw.shape[-2:], boxes)
+        block = (dw.shape[-2], SEG // 2)
+        for spot, order in enumerate(FEED_ORDERS):
+            columns = pl.ds(spot % 2 * block[1], block[1])
+            source = dw.at[2 + spot // 2, :, :, :, :, :, columns]
+            run = Scatter(place, source, "yzx", order, {}, hands.at[spot], (send.at[spot], recv.at[spot]))
+            open_inbox(run, place.count, "yzx", order, block, boxes)
             runs.append(run)
         swap = Swap(place, mover, ysem, side.wait, half_out, pair)
-        comm = {0: runs[0].steps(), 1: runs[1].steps(), 2: swap.steps(0) + swap.steps(1)}
+        comm = {spot: run.steps() for spot, run in enumerate(runs)}
+        comm[len(runs)] = swap.steps(0) + swap.steps(1)
 
     def down_grad(which):
         if which == 0:
@@ -876,9 +899,9 @@
     pieces += [last, mix_grad, lambda: turn(gl, glt), out_grad]
     play(FEED_PLAN, comm, pieces)
     if shape:
-        for which in range(2):
-            grad_down[:, which * SEG : (which + 1) * SEG] = runs[which].result().astype(F32)
-            runs[which].drain()
+        for spot, run in enumerate(runs):
+            grad_down[:, spot * block[1] : (spot + 1) * block[1]] = run.result().astype(F32)
+            run.drain()
         swap.wait()
     mover.close()
 
@@ -997,9 +1020,9 @@
     def before_heads():
         loads["nrmt"].wait()
 
-    pieces = [ready, (3, mixing), before_heads]
+    pieces = [ready, (3, mixing, None, None), before_heads]
     parts = [functools.partial(token_grad, part) for part in range(micro)]
-    heads = [(3, head_grad)]
+    heads = [(3, head_grad, None, None)]
     pieces += heads + parts if GRADS_FIRST else parts + heads
     pieces.insert(len(pieces) - (0 if GRADS_FIRST else 1), spread_vectors)
     play(ATTN_PLAN, comm, pieces)
@@ -1023,6 +1046,16 @@
         vec_out[...] = tiles[place.at["z"], place.at["x"]] + ybox[...]
         swap.wait()
     mover.close()
+
+
+def finish_kernel(low, *refs):
+    grads, tokens, outs = refs[:6], refs[6], refs[7:]
+    tokens[...] = low[...].astype(F32)
+
+    @pl.when((pl.program_id(0) == 0) & (pl.program_id(1) == 0))
+    def _():
+        for grad, out in zip(grads, outs):
+            out[...] = grad[...]
 
 
 def shape_of(shape, dtype):
@@ -1087,7 +1120,8 @@
     count = dict(zip("zxy", shape))
     slots = link_slots(count, "zxy")
     scratch += [pltpu.VMEM(shape[:2] + (2, 8, 128), F32)]
-    scratch += [DMA((9, slots)), DMA((9, slots)), DMA((9, slots + 1)), DMA((9, slots + 1))]
+    runs = len(ORDERS) + 1
+    scratch += [DMA((runs, slots)), DMA((runs, slots)), DMA((runs, slots + 1)), DMA((runs, slots + 1))]
     results = call(
         functools.partial(forward_kernel, shape, micro),
         (shape_of(full, BF), shape_of((8, width), F32)) + saved,
@@ -1100,8 +1134,8 @@
     return results[0], results[1], dict(zip(FWD_OUT, results[2:]))
 
 
-def scatter_scratch(segs, part, count, orders):
-    rows, cols = part.shape[-2:]
+def scatter_scratch(segs, part, count, orders, cols=SEG):
+    rows = part.shape[-2]
     slots = link_slots(count, "zxy") + 1
     boxes = []
     for order in orders:
@@ -1143,7 +1177,7 @@
     specs = [ANYWHERE, ANYWHERE, ANYWHERE, IN_VMEM]
     if shape:
         count = dict(zip("zxy", shape))
-        hands, sems, boxes = scatter_scratch(2, part, count, [BACK_ORDERS[seg] for seg in DOWNS])
+        hands, sems, boxes = scatter_scratch(len(FEED_ORDERS), part, count, FEED_ORDERS, SEG // 2)
         scratch += [vmem(raw), hands] + sems + [DMA((8,))] + boxes
         outs += [pair_of(raw, shape[2]), shape_of((part.shape[-2], 2 * SEG), F32)]
         specs += [ANYWHERE, IN_VMEM]
@@ -1191,6 +1225,22 @@
     )(vectors, vec_f, g, dw_in, *(kept[name] for name in BACK_IN))
 
 
+def finish(low, grads):
+    parts, patches, series, width = low.shape
+    cuts = 3 if patches % 3 == 0 else 1
+    block = pl.BlockSpec((1, patches // cuts, series, width), lambda part, cut: (part, cut, 0, 0))
+    whole = [pl.BlockSpec(grad.shape, lambda part, cut: (0, 0)) for grad in grads]
+    return pl.pallas_call(
+        finish_kernel,
+        grid=(parts, cuts),
+        out_shape=[shape_of(low.shape, F32)] + [shape_of(grad.shape, F32) for grad in grads],
+        in_specs=[block] + whole,
+        out_specs=[block] + whole,
+        compiler_params=pltpu.CompilerParams(vmem_limit_bytes=VMEM_LIMIT),
+        name="finish",
+    )(low, *grads)
+
+
 def chip_grid(chips):
     nx = 1
     while (nx * 2) ** 2 <= chips:
@@ -1226,7 +1276,7 @@
     if linked:
         out, grad_down = results[4:]
         grad_tokens, *grads, vec = attn_back(shape, vectors, vec_f, g, dw_f, kept)
-        grads.append(grad_down)
+        grad_tokens, *grads = finish(grad_tokens, grads + [grad_down])
         core = lax.rem(lax.axis_index("dp"), 2)
         vec = lax.dynamic_slice(vec, (0, core * share), (4, share))
     else:

time: 217 us -> 215 us (level)
  other arithmetic: 5.27 us -> 0 us
  Pallas kernels: 205 us -> 209 us
    pallas_call x0 -> x1, Pallas kernels: none -> 9.32 us  [finish(): pl.pallas_call(finish_kernel, grid=(parts, cuts), out_shape=[shape_of(low...]
    pallas_call x1, Pallas kernels: 48.4 us -> 41.2 us  [feed_back(): call(functools.partial(feed_back_kernel, shape), tuple(outs), [IN_VMEM] +...]
    transpose x1 -> x0, other arithmetic: 5.27 us -> none  [body(): flip = lambda array: jnp.transpose(array, (0, 2, 1, 3))]
    unnamed x23 -> x3, local copies, waits for them, and re-layouts: 5.66 us -> 3.72 us
where the time goes in v3:
time: 215 us; the launch traced here: 214 us
  Pallas kernels  209 us (97%)
  local copies, waits for them, and re-layouts  4.32 us (2%)
    pallas_call x1, Pallas kernels, forward(): call(functools.partial(forward_kernel, shape, micro), (shape_of(full, BF)...  84.8 us
    pallas_call x1, Pallas kernels, attn_back(): call(functools.partial(attn_back_kernel, shape), tuple(outs), [IN_VMEM] *...  73.7 us
    pallas_call x1, Pallas kernels, feed_back(): call(functools.partial(feed_back_kernel, shape), tuple(outs), [IN_VMEM] +...  41.2 us
    pallas_call x1, Pallas kernels, finish(): pl.pallas_call(finish_kernel, grid=(parts, cuts), out_shape=[shape_of(low...  9.32 us

profile of v3, /device:TPU:0, one launch (start us, length us, event | category | flops | bytes accessed | tf_op | source)
XLA Modules:
  0.0 214.1 jit_solution(17650313660166337416)
XLA Ops:
  0.6 84.8 %forward.1 = (bf16[8,2,4,2,2,64,512]{6,5,4,3,2,1,0:T(8,128)(2,1)}, f32[8,1024]{1,0:T(8,128)}, bf16[768,1024]{1,0:T(8,128)(2,1)}, bf16[768,1024]{1,0:T(8,128)(2,1...) custom-call(bf16[4,15,24,1024]{3,2,1,0:T(8,128)(2,1)} %bitcast.16, ...), custom_call_target="tpu_custom_call" | custom-call | tf_op jit(solution)/shard_map/forward/pallas_call | solution.py:1125
  85.5 41.2 %feed_back.1 = (bf16[5,2,4,2,2,64,512]{6,5,4,3,2,1,0:T(8,128)(2,1)}, f32[768,1024]{1,0:T(8,128)}, bf16[768,1024]{1,0:T(8,128)(2,1)}, f32[2,8,1024]{2,1,0:T(8,128...) custom-call(f32[8,1024]{1,0:T(8,128)} %get-tuple-element.50.vectors, ...), custom_call_target="tpu_custom_call" | custom-call | tf_op jit(solution)/shard_map/feed_back/pallas_call | solution.py:1184
  126.7 73.7 %attn_back.1 = (bf16[4,15,24,1024]{3,2,1,0:T(8,128)(2,1)}, f32[64,512]{1,0:T(8,128)}, f32[64,512]{1,0:T(8,128)}, f32[64,512]{1,0:T(8,128)}, f32[64,512]{1,0:T(8,...) custom-call(f32[8,1024]{1,0:T(8,128)} %get-tuple-element.50.vectors, f32[2,8,1024]{2,1,0:T(8,128)} %get-tuple-element.63.vec_f, ...), custom_call_target="tpu_custom_call" | custom-call | tf_op jit(solution)/shard_map/attn_back/pallas_call | solution.py:1217
  200.4 0.0 copy-start
  200.4 9.3 %finish.1 = (f32[4,15,24,1024]{3,2,1,0:T(8,128)}, f32[64,512]{1,0:T(8,128)}, f32[64,512]{1,0:T(8,128)}, f32[64,512]{1,0:T(8,128)}, f32[64,512]{1,0:T(8,128)}, /*index=5*/f32[64,1024]{1,0:T(8,128)}, f32[64,1024]{1,0:T(8,128)}) custom-call(bf16[4,15,24,1024]{3,2,1,0:T(8,128)(2,1)} %get-tuple-element.73.low, f32[64,512]{1,0:T(8,128)} %get-tuple-element.74.refs_0_, ...), custom_call_target="tpu_custom_call" | custom-call | tf_op jit(solution)/shard_map/finish/pallas_call | solution.py:1233
  209.8 0.0 copy-done
  209.8 0.1 constant_dynamic-slice_fusion
  209.8 0.5 slice_bitcast_fusion
  210.4 3.7 %copy.27 = bf16[4,24,15,1024]{3,1,2,0:T(8,128)(2,1)} copy(bf16[4,24,15,1024]{3,1,2,0:T(8,128)(2,1)} %bitcast.18) | data formatting | bytes 5898240
Async XLA Ops:
  200.4 9.3 %copy-start = (f32[8,128]{1,0:T(8,128)S(1)}, f32[8,128]{1,0:T(8,128)}, u32[]{:S(2)}) copy-start(f32[8,128]{1,0:T(8,128)} %get-tuple-element.87) | copy-start | bytes 12292

commit v4 on v3

--- a/solution.py
+++ b/solution.py
@@ -20,16 +20,14 @@
 Q, K, V, O, U0, U1, D0, D1 = range(8)
 UPS = (U0, U1)
 DOWNS = (D0, D1)
-ORDERS = ("zxy", "zxy", "zyx", "zyx", "zxy", "zyx", "yzx", "zxy", "yxz", "zxy", "zyx", "yxz", "xzy", "zxy", "xyz", "yzx")
+ORDERS = ("zyx", "zxy", "zxy", "yzx", "xyz", "zxy", "zyx", "xyz")
 BACK_ORDERS = ("yxz", "xzy", "xzy", "zxy", "xzy", "yxz")
 FEED_ORDERS = ("xzy", "zxy", "zxy", "xzy")
 
 FORWARD_PLAN = (
-    3, 14, 7, 6, 5, 11, -1, 8, 15, 3, 7, 14, 11, 0, 10, 8, 12, 3, 3, 7, 5, 7, 0, 5,
-    0, 16, 4, 5, 1, 9, 0, 13, 16, 3, 7, 4, 1, 16, 16, 2, 6, 0, 1, 4, 13, 2, 13, 10,
-    1, 9, 4, 2, 15, 9, 16, 12, 6, 2, 1, 5, 7, 8, -1, -1, 3, 12, 2, 10, 6, 15, 4, 11,
-    0, 12, 5, 10, 9, 1, 8, 6, 13, -1, 2, 12, 4, 9, 11, -1, 14, -1, 10, -1, 6, 8, 15, -1,
-    12, -1, 11, 14, 13, -1, 15, 8, 9, -1, 11, 10, -1, -1, 14, -1, 13, -1, 15, 14, -1, -1, -1,
+    2, 1, 8, 4, 0, 3, 4, 2, 7, 8, -1, 0, 2, 7, 8, 1, 2, 0, 6, 0, 1, 5, 3, 1,
+    2, 8, 5, 4, 0, 5, 8, 6, -1, 6, 3, 1, 5, 3, 3, 0, 4, -1, 2, 6, -1, 4, 1, 5,
+    7, -1, -1, 6, -1, 4, 3, -1, 7, -1, -1, -1, -1, 5, 7, -1, -1, 6, -1, 7, -1, -1, -1,
 )
 FEED_PLAN = (
     4, -1, 1, -1, 1, 0, -1, 3, 4, 0, 4, 1, 2, -1, 2, 3, -1, 1, -1, 0, 2, -1, 1, 0,
@@ -346,20 +344,14 @@
                 def _(dim=dim, t=t, way=way, position=position):
                     self.hand(self.slots[dim, t, way], dim, position, other).wait_recv()
 
-    def drain(self):
+    def drain_hand(self):
         self.hand(len(self.slots), "", None, self.place.core).wait_send()
-        for dim, t in self.rounds:
-            for way, position, valid in self.sends(dim, t):
-
-                @pl.when(valid)
-                def _(dim=dim, t=t, way=way, position=position):
-                    self.link(dim, t, way, position, self.place.partner()).wait_send()
-
-            for way, position, valid in self.arrivals(dim, t):
-
-                @pl.when(valid)
-                def _(dim=dim, t=t, way=way, position=position):
-                    self.hand(self.slots[dim, t, way], dim, position, self.place.core).wait_send()
+
+    def sent(self, dim, t):
+        for way, position, valid in self.sends(dim, t):
+            yield valid, self.link(dim, t, way, position, self.place.partner())
+        for way, position, valid in self.arrivals(dim, t):
+            yield valid, self.hand(self.slots[dim, t, way], dim, position, self.place.core)
 
 
 class Scatter:
@@ -466,15 +458,26 @@
     def result(self):
         return self.mine[self.own(tuple(self.place.at[axis] for axis in self.axes))]
 
-    def drain(self):
+    def drain_hand(self):
         if not self.both:
             self.hand().wait_send()
-        for dim, t in self.rounds:
-            for way, position, valid in self.sends(dim, t):
-
-                @pl.when(valid)
-                def _(dim=dim, t=t, way=way, position=position):
-                    self.link(dim, t, way, position, self.place.partner()).wait_send()
+
+    def sent(self, dim, t):
+        for way, position, valid in self.sends(dim, t):
+            yield valid, self.link(dim, t, way, position, self.place.partner())
+
+
+def drain(runs):
+    for run in runs:
+        run.drain_hand()
+    for dim, t in dict.fromkeys(key for run in runs for key in run.rounds):
+        groups = [list(run.sent(dim, t)) for run in runs if (dim, t) in run.rounds]
+        for same in zip(*groups):
+
+            @pl.when(same[0][0])
+            def _(same=same):
+                for _valid, copy in same:
+                    copy.wait_send()
 
 
 def inbox_shapes(count, axes, order, block):
@@ -731,8 +734,7 @@
     pieces += [functools.partial(down, which) for which in range(2)] + [last]
     play(FORWARD_PLAN, comm, pieces)
     if shape:
-        for run in runs:
-            run.drain()
+        drain(runs)
     mover.close()
 
 
@@ -901,7 +903,7 @@
     if shape:
         for spot, run in enumerate(runs):
             grad_down[:, spot * block[1] : (spot + 1) * block[1]] = run.result().astype(F32)
-            run.drain()
+        drain(runs)
         swap.wait()
     mover.close()
 
@@ -926,7 +928,7 @@
     given = dict(zip(BACK_IN, refs[:8]))
     refs = refs[8:]
     if shape:
-        pair, grads, vec_out, refs = refs[0], refs[1:6], refs[6], refs[7:]
+        grad_down, pair, packed, vec_out, refs = refs[:4] + (refs[4:],)
     else:
         dw_out, out, vec, refs = refs[0], refs[1], refs[2], refs[3:]
     here = dict(zip(BACK_IN, refs[:8]))
@@ -1036,26 +1038,14 @@
             here_tile, ybox, ysem.at[8], ysem.at[9], device_id=place.device(y=1 - place.at["y"]), device_id_type=MESH
         )
         copy.start()
-        for spot, seg in enumerate(SHARED[2:]):
-            grads[(3, 0, 1, 2)[spot]][...] = runs[2 + spot].result().astype(F32)
-        for which in range(2):
-            grads[4][:, which * SEG : (which + 1) * SEG] = runs[which].result().astype(F32)
-        for run in runs:
-            run.drain()
+        packed[:, 6 * SEG :] = grad_down[...]
+        for spot, column in enumerate((4, 5, 3, 0, 1, 2)):
+            packed[:, column * SEG : (column + 1) * SEG] = runs[spot].result().astype(F32)
+        drain(runs)
         copy.wait()
         vec_out[...] = tiles[place.at["z"], place.at["x"]] + ybox[...]
         swap.wait()
     mover.close()
-
-
-def finish_kernel(low, *refs):
-    grads, tokens, outs = refs[:6], refs[6], refs[7:]
-    tokens[...] = low[...].astype(F32)
-
-    @pl.when((pl.program_id(0) == 0) & (pl.program_id(1) == 0))
-    def _():
-        for grad, out in zip(grads, outs):
-            out[...] = grad[...]
 
 
 def shape_of(shape, dtype):
@@ -1192,7 +1182,7 @@
     )(vectors, *given)
 
 
-def attn_back(shape, vectors, vec_f, g, dw_in, kept):
+def attn_back(shape, vectors, vec_f, g, dw_in, kept, grad_down=None):
     low, raw = kept["x"], kept["out"]
     width = low.shape[1]
     part = shape_of((3,) + g.shape[1:], BF)
@@ -1203,9 +1193,8 @@
         nz, nx, ny = shape
         count = dict(zip("zxy", shape))
         share = part.shape[-2]
-        small, large = shape_of((share, SEG), F32), shape_of((share, 2 * SEG), F32)
-        outs = [pair_of(raw, ny)] + [small] * 4 + [large, shape_of((8, 128), F32)]
-        specs = [ANYWHERE] + [IN_VMEM] * 6
+        outs = [pair_of(raw, ny), shape_of((share, 8 * SEG), F32), shape_of((8, 128), F32)]
+        specs = [ANYWHERE] + [IN_VMEM] * 2
         hands, sems, boxes = scatter_scratch(7, part, count, [BACK_ORDERS[seg] for seg in SHARED])
         tiles = pltpu.VMEM((nz, nx, 8, 128), F32)
         scratch += [vmem(part), tiles, hands, tiles, pltpu.VMEM((8, 128), F32), vmem(vec)]
@@ -1217,28 +1206,12 @@
     return call(
         functools.partial(attn_back_kernel, shape),
         tuple(outs),
-        [IN_VMEM] * 2 + [ANYWHERE] * 10,
+        [IN_VMEM] * 2 + [ANYWHERE] * 10 + ([IN_VMEM] if shape else []),
         tuple(specs),
         scratch,
         "attn_back",
         2 if shape else None,
-    )(vectors, vec_f, g, dw_in, *(kept[name] for name in BACK_IN))
-
-
-def finish(low, grads):
-    parts, patches, series, width = low.shape
-    cuts = 3 if patches % 3 == 0 else 1
-    block = pl.BlockSpec((1, patches // cuts, series, width), lambda part, cut: (part, cut, 0, 0))
-    whole = [pl.BlockSpec(grad.shape, lambda part, cut: (0, 0)) for grad in grads]
-    return pl.pallas_call(
-        finish_kernel,
-        grid=(parts, cuts),
-        out_shape=[shape_of(low.shape, F32)] + [shape_of(grad.shape, F32) for grad in grads],
-        in_specs=[block] + whole,
-        out_specs=[block] + whole,
-        compiler_params=pltpu.CompilerParams(vmem_limit_bytes=VMEM_LIMIT),
-        name="finish",
-    )(low, *grads)
+    )(vectors, vec_f, g, dw_in, *(kept[name] for name in BACK_IN), *((grad_down,) if shape else ()))
 
 
 def chip_grid(chips):
@@ -1275,8 +1248,9 @@
     kept = {**kept, "gres": gres, "gm": gm}
     if linked:
         out, grad_down = results[4:]
-        grad_tokens, *grads, vec = attn_back(shape, vectors, vec_f, g, dw_f, kept)
-        grad_tokens, *grads = finish(grad_tokens, grads + [grad_down])
+        grad_tokens, packed, vec = attn_back(shape, vectors, vec_f, g, dw_f, kept, grad_down)
+        cuts = [0, SEG, 2 * SEG, 3 * SEG, 4 * SEG, 6 * SEG, 8 * SEG]
+        grads = [packed[:, start:stop] for start, stop in zip(cuts, cuts[1:])]
         core = lax.rem(lax.axis_index("dp"), 2)
         vec = lax.dynamic_slice(vec, (0, core * share), (4, share))
     else:

time: 215 us -> 210 us (0.977)
  Pallas kernels: 209 us -> 200 us
  other arithmetic: 0 us -> 5.27 us
    pallas_call x1 -> x0, Pallas kernels: 9.32 us -> none  [finish(): pl.pallas_call(finish_kernel, grid=(parts, cuts), out_shape=[shape_of(low...]
    transpose x0 -> x1, other arithmetic: none -> 5.27 us  [body(): flip = lambda array: jnp.transpose(array, (0, 2, 1, 3))]
where the time goes in v4:
time: 210 us
  Pallas kernels  200 us (95%)
  other arithmetic  5.27 us (3%)
  local copies, waits for them, and re-layouts  3.85 us (2%)
    pallas_call x1, Pallas kernels, forward(): call(functools.partial(forward_kernel, shape, micro), (shape_of(full, BF)...  82.8 us
    pallas_call x1, Pallas kernels, attn_back(): call(functools.partial(attn_back_kernel, shape), tuple(outs), [IN_VMEM] *...  74.9 us
    pallas_call x1, Pallas kernels, feed_back(): call(functools.partial(feed_back_kernel, shape), tuple(outs), [IN_VMEM] +...  42.7 us
    transpose x1, other arithmetic, body(): flip = lambda array: jnp.transpose(array, (0, 2, 1, 3))  5.27 us

profile of v4, /device:TPU:0, one launch (start us, length us, event | category | flops | bytes accessed | tf_op | source)
XLA Modules:
  0.0 210.2 jit_solution(4500756670209738496)
XLA Ops:
  0.6 82.8 %forward.1 = (bf16[8,2,4,2,2,64,512]{6,5,4,3,2,1,0:T(8,128)(2,1)}, f32[8,1024]{1,0:T(8,128)}, bf16[768,1024]{1,0:T(8,128)(2,1)}, bf16[768,1024]{1,0:T(8,128)(2,1...) custom-call(bf16[4,15,24,1024]{3,2,1,0:T(8,128)(2,1)} %bitcast.17, ...), custom_call_target="tpu_custom_call" | custom-call | tf_op jit(solution)/shard_map/forward/pallas_call | solution.py:1115
  83.5 42.7 %feed_back.1 = (bf16[5,2,4,2,2,64,512]{6,5,4,3,2,1,0:T(8,128)(2,1)}, f32[768,1024]{1,0:T(8,128)}, bf16[768,1024]{1,0:T(8,128)(2,1)}, f32[2,8,1024]{2,1,0:T(8,128...) custom-call(f32[8,1024]{1,0:T(8,128)} %get-tuple-element.39.vectors, ...), custom_call_target="tpu_custom_call" | custom-call | tf_op jit(solution)/shard_map/feed_back/pallas_call | solution.py:1174
  126.2 74.9 %attn_back.1 = (bf16[4,15,24,1024]{3,2,1,0:T(8,128)(2,1)}, f32[64,4096]{1,0:T(8,128)}, f32[8,128]{1,0:T(8,128)}) custom-call(f32[8,1024]{1,0:T(8,128)} %get-tuple-element.39.vectors, f32[2,8,1024]{2,1,0:T(8,128)} %get-tuple-element.52.vec_f, bf16[8,2,4,2,2,64,512]{6,5,4,3,2,1,0:T(8,128)(2,1)} %get-tuple-element.40.g_in, ...), custom_call_target="tpu_custom_call" | custom-call | tf_op jit(solution)/shard_map/attn_back/pallas_call | solution.py:1206
  201.1 0.0 copy-start.1
  201.1 0.0 copy-start.2
  201.1 0.0 copy-start
  201.1 5.3 %convert_bitcast_fusion = f32[4,24,15,1024]{3,1,2,0:T(8,128)} fusion(bf16[4,15,24,1024]{3,2,1,0:T(8,128)(2,1)} %get-tuple-element.63), kind=kLoop, calls=%fused_computation | loop fusion | flops 1474560 | bytes 8847360 | tf_op jit(solution)/shard_map/transpose | solution.py:1232
  206.4 0.0 copy-done.1
  206.4 0.8 fusion.1
  207.2 0.8 fusion
  208.0 0.0 copy-done.2
  208.0 0.1 constant_dynamic-slice_fusion
  208.1 0.5 slice_bitcast_fusion
  208.6 0.0 copy-done
  208.6 1.6 copy.27
Async XLA Ops:
  201.1 5.3 %copy-start.1 = (f32[64,4096]{1,0:T(8,128)S(1)}, f32[64,4096]{1,0:T(8,128)}, u32[]{:S(2)}) copy-start(f32[64,4096]{1,0:T(8,128)} %get-tuple-element.64) | copy-start | bytes 3145732
  201.1 6.9 %copy-start.2 = (f32[8,128]{1,0:T(8,128)S(1)}, f32[8,128]{1,0:T(8,128)}, u32[]{:S(2)}) copy-start(f32[8,128]{1,0:T(8,128)} %get-tuple-element.65) | copy-start | bytes 12292
  201.1 7.5 %copy-start = (bf16[4,15,24,1024]{3,2,1,0:T(8,128)(2,1)S(1)}, bf16[4,15,24,1024]{3,2,1,0:T(8,128)(2,1)}, u32[]{:S(2)}) copy-start(bf16[4,15,24,1024]{3,2,1,0:T(8,128)(2,1)} %get-tuple-element.51) | copy-start | bytes 8847364

commit v5 on v4

--- a/solution.py
+++ b/solution.py
@@ -20,23 +20,24 @@
 Q, K, V, O, U0, U1, D0, D1 = range(8)
 UPS = (U0, U1)
 DOWNS = (D0, D1)
-ORDERS = ("zyx", "zxy", "zxy", "yzx", "xyz", "zxy", "zyx", "xyz")
-BACK_ORDERS = ("yxz", "xzy", "xzy", "zxy", "xzy", "yxz")
-FEED_ORDERS = ("xzy", "zxy", "zxy", "xzy")
+ORDERS = ("zxy", "zyx", "zxy", "xyz", "yzx", "zxy", "zyx", "xyz")
+BACK_ORDERS = ("zxy", "xzy", "yxz", "xyz", "xzy", "zxy", "yxz", "xzy", "xzy")
+FEED_ORDERS = ("zxy", "xzy", "zxy", "xzy")
 
 FORWARD_PLAN = (
-    2, 1, 8, 4, 0, 3, 4, 2, 7, 8, -1, 0, 2, 7, 8, 1, 2, 0, 6, 0, 1, 5, 3, 1,
-    2, 8, 5, 4, 0, 5, 8, 6, -1, 6, 3, 1, 5, 3, 3, 0, 4, -1, 2, 6, -1, 4, 1, 5,
-    7, -1, -1, 6, -1, 4, 3, -1, 7, -1, -1, -1, -1, 5, 7, -1, -1, 6, -1, 7, -1, -1, -1,
+    0, 1, 4, 3, 0, 8, 2, 7, 3, -1, 0, 1, 0, 8, 7, 1, 2, 1, 8, 8, 2, 2, 5, 6,
+    0, 4, 1, 5, 2, 6, 5, 6, 4, 3, 5, -1, 6, 4, 8, 4, 0, 3, -1, 1, -1, 2, 5, 3,
+    7, -1, -1, -1, 3, 6, -1, -1, -1, 7, -1, 4, -1, 5, -1, 7, -1, 6, -1, -1, 7, -1, -1,
 )
 FEED_PLAN = (
-    4, -1, 1, -1, 1, 0, -1, 3, 4, 0, 4, 1, 2, -1, 2, 3, -1, 1, -1, 0, 2, -1, 1, 0,
-    -1, 3, 1, 4, 2, -1, 3, 1, -1, 0, 2, 3, -1, 0, -1, 2, 3, -1, 0, 2, 3,
+    4, -1, 0, 4, -1, 0, 1, -1, 0, 2, 1, 3, -1, 2, -1, 4, -1, 4, 3, 2, 0, -1, -1, 1,
+    -1, 1, 0, 3, 2, -1, 3, -1, 1, 2, 3, 1, 0, -1, 2, 3, -1, 0, 2, 1, 3,
 )
 ATTN_PLAN = (
-    0, 1, -1, 1, 0, -1, 2, -1, -1, -1, -1, 3, 2, -1, 4, 3, -1, 2, 4, 0, 5, -1, 7, 0,
-    5, 1, 0, 7, 3, 2, 4, -1, 8, -1, 0, 4, 5, 5, 8, 6, 6, 1, 4, 6, 5, 2, 6, 4,
-    3, 1, 5, 6, 3, 1, 2, 6, 3, 5, 1, 4, 0, 3, 2,
+    2, 0, -1, -1, 2, 1, 0, -1, -1, 1, -1, -1, -1, 0, 4, 6, 5, -1, 8, 5, 6, -1, 10, 8,
+    0, 7, 4, -1, -1, 1, 3, 3, 10, 1, 7, 2, 9, 9, 8, 9, 8, 11, 9, 1, 4, 3, 4, 5,
+    8, 5, 1, 7, 6, 0, 11, 4, 3, 2, 9, 8, 6, 4, 7, 3, 2, 7, 5, 0, 6, 9, 2, 3,
+    5, 6, 7, 1, 4, 8, 0, 5, 2, 3, 7, 6,
 )
 GRADS_FIRST = 1
 
@@ -920,8 +921,9 @@
 
 
 BACK_IN = ("gm", "q", "k", "v", "probs", "nrmt", "gres", "x")
-SHARED = (U0, U1, O, Q, K, V)
 KEPT_GRADS = (0, 1, 4)
+HALF = SEG // 2
+SPOTS = (4 * SEG, 5 * SEG, 3 * SEG, 0, HALF, SEG, SEG + HALF, 2 * SEG, 2 * SEG + HALF)
 
 
 def attn_back_kernel(shape, vectors, vec_f, g_in, dw_in, *refs):
@@ -936,8 +938,8 @@
     mover = Mover(sems)
     loads, comm = {}, {}
     if shape:
-        held, tiles, hands, vec_hand, ybox, vec, send, recv, ysem = refs[14:23]
-        boxes = list(refs[23:])
+        held, tiles, hands, half_hands, vec_hand, ybox, vec, send, recv, ysem = refs[14:24]
+        boxes = list(refs[24:])
 
     def fetch_held(*spots):
         for spot in spots:
@@ -945,9 +947,13 @@
                 loads["dw", spot] = mover.start(dw_in.at[KEPT_GRADS[spot]], held.at[spot])
 
     fetch_held(0)
-    for name in BACK_IN[:5]:
-        loads[name] = mover.start(given[name], here[name])
-    fetch_held(1, 2)
+    some = here["gm"].shape[0] // 3
+    for part in range(3):
+        rows = pl.ds(part * some, some)
+        for name in BACK_IN[:5]:
+            loads[name, part] = mover.start(given[name].at[rows], here[name].at[rows])
+        if part == 0:
+            fetch_held(1, 2)
     for name in BACK_IN[5:]:
         loads[name] = mover.start(given[name], here[name])
     for seg in (Q, K, V):
@@ -958,18 +964,23 @@
         place = Place(shape)
         place.barrier("zxy")
         runs = []
-        for spot, seg in enumerate(SHARED):
-            source = held.at[spot] if spot < 3 else dw.at[seg]
-            order = BACK_ORDERS[seg]
-            run = Scatter(place, source, "yzx", order, {}, hands.at[spot], (send.at[spot], recv.at[spot]))
-            open_inbox(run, place.count, "yzx", order, dw.shape[-2:], boxes)
+        for spot, order in enumerate(BACK_ORDERS):
+            sems_of = (send.at[spot], recv.at[spot])
+            if spot < 3:
+                width, source, hand = SEG, held.at[spot], hands.at[spot]
+            else:
+                seg, side = (spot - 3) // 2, (spot - 3) % 2
+                width, hand = HALF, half_hands.at[spot - 3]
+                source = dw.at[seg, :, :, :, :, :, pl.ds(side * HALF, HALF)]
+            run = Scatter(place, source, "yzx", order, {}, hand, sems_of)
+            open_inbox(run, place.count, "yzx", order, (dw.shape[-2], width), boxes)
             runs.append(run)
-        run = Scatter(place, tiles, "zx", "zx", {}, vec_hand, (send.at[6], recv.at[6]), both=True)
+        run = Scatter(place, tiles, "zx", "zx", {}, vec_hand, (send.at[9], recv.at[9]), both=True)
         open_inbox(run, {"z": place.nz, "x": place.nx}, "zx", "zx", (8, 128), boxes)
         runs.append(run)
         swap = Swap(place, mover, ysem, lambda: None, raw, pair)
         comm = {spot: run.steps() for spot, run in enumerate(runs)}
-        comm[7], comm[8] = swap.steps(0), swap.steps(1)
+        comm[10], comm[11] = swap.steps(0), swap.steps(1)
         for spot in range(3):
             comm[spot][0] = lambda spot=spot: (loads["dw", spot].wait(), runs[spot].start())
 
@@ -978,11 +989,16 @@
     share = gal.shape[0] // micro
 
     def ready():
-        for name in BACK_IN[:5]:
-            loads[name].wait()
         vec[...] = jnp.zeros_like(vec)
 
     def mixing(part):
+        for third_of in range(3):
+
+            @pl.when(part == third_of)
+            def _(third_of=third_of):
+                for name in BACK_IN[:5]:
+                    loads[name, third_of].wait()
+
         attend_back(q, k, v, probs, gm, pulls.at[0], pulls.at[1], pulls.at[2], part * third, third)
 
     def head_grad(seg):
@@ -1039,8 +1055,9 @@
         )
         copy.start()
         packed[:, 6 * SEG :] = grad_down[...]
-        for spot, column in enumerate((4, 5, 3, 0, 1, 2)):
-            packed[:, column * SEG : (column + 1) * SEG] = runs[spot].result().astype(F32)
+        for spot, column in enumerate(SPOTS):
+            width = SEG if spot < 3 else HALF
+            packed[:, column : column + width] = runs[spot].result().astype(F32)
         drain(runs)
         copy.wait()
         vec_out[...] = tiles[place.at["z"], place.at["x"]] + ybox[...]
@@ -1195,9 +1212,11 @@
         share = part.shape[-2]
         outs = [pair_of(raw, ny), shape_of((share, 8 * SEG), F32), shape_of((8, 128), F32)]
         specs = [ANYWHERE] + [IN_VMEM] * 2
-        hands, sems, boxes = scatter_scratch(7, part, count, [BACK_ORDERS[seg] for seg in SHARED])
+        hands, sems, boxes = scatter_scratch(10, part, count, BACK_ORDERS[:3])
+        half_hands, _, more = scatter_scratch(10, part, count, BACK_ORDERS[3:], HALF)
+        boxes += more
         tiles = pltpu.VMEM((nz, nx, 8, 128), F32)
-        scratch += [vmem(part), tiles, hands, tiles, pltpu.VMEM((8, 128), F32), vmem(vec)]
+        scratch += [vmem(part), tiles, hands, half_hands, tiles, pltpu.VMEM((8, 128), F32), vmem(vec)]
         scratch += sems + [DMA((10,))] + boxes
         scratch += [pltpu.VMEM(s, F32) for s in inbox_shapes({"z": nz, "x": nx}, "zx", "zx", (8, 128))[0]]
     else:

time: 210 us -> 212 us (level)
  no operation moved by 1% of the time
where the time goes in v5:
time: 212 us
  Pallas kernels  202 us (95%)
  other arithmetic  5.27 us (2%)
  local copies, waits for them, and re-layouts  3.85 us (2%)
    pallas_call x1, Pallas kernels, forward(): call(functools.partial(forward_kernel, shape, micro), (shape_of(full, BF)...  84.3 us
    pallas_call x1, Pallas kernels, attn_back(): call(functools.partial(attn_back_kernel, shape), tuple(outs), [IN_VMEM] *...  75.8 us
    pallas_call x1, Pallas kernels, feed_back(): call(functools.partial(feed_back_kernel, shape), tuple(outs), [IN_VMEM] +...  42.4 us
    transpose x1, other arithmetic, body(): flip = lambda array: jnp.transpose(array, (0, 2, 1, 3))  5.27 us

profile of v5, /device:TPU:0, one launch (start us, length us, event | category | flops | bytes accessed | tf_op | source)
XLA Modules:
  0.0 212.3 jit_solution(10838604635897215324)
XLA Ops:
  0.6 84.3 %forward.1 = (bf16[8,2,4,2,2,64,512]{6,5,4,3,2,1,0:T(8,128)(2,1)}, f32[8,1024]{1,0:T(8,128)}, bf16[768,1024]{1,0:T(8,128)(2,1)}, bf16[768,1024]{1,0:T(8,128)(2,1...) custom-call(bf16[4,15,24,1024]{3,2,1,0:T(8,128)(2,1)} %bitcast.17, ...), custom_call_target="tpu_custom_call" | custom-call | tf_op jit(solution)/shard_map/forward/pallas_call | solution.py:1132
  85.0 42.4 %feed_back.1 = (bf16[5,2,4,2,2,64,512]{6,5,4,3,2,1,0:T(8,128)(2,1)}, f32[768,1024]{1,0:T(8,128)}, bf16[768,1024]{1,0:T(8,128)(2,1)}, f32[2,8,1024]{2,1,0:T(8,128...) custom-call(f32[8,1024]{1,0:T(8,128)} %get-tuple-element.39.vectors, ...), custom_call_target="tpu_custom_call" | custom-call | tf_op jit(solution)/shard_map/feed_back/pallas_call | solution.py:1191
  127.3 75.8 %attn_back.1 = (bf16[4,15,24,1024]{3,2,1,0:T(8,128)(2,1)}, f32[64,4096]{1,0:T(8,128)}, f32[8,128]{1,0:T(8,128)}) custom-call(f32[8,1024]{1,0:T(8,128)} %get-tuple-element.39.vectors, f32[2,8,1024]{2,1,0:T(8,128)} %get-tuple-element.52.vec_f, bf16[8,2,4,2,2,64,512]{6,5,4,3,2,1,0:T(8,128)(2,1)} %get-tuple-element.40.g_in, ...), custom_call_target="tpu_custom_call" | custom-call | tf_op jit(solution)/shard_map/attn_back/pallas_call | solution.py:1225
  203.1 0.0 copy-start.1
  203.1 0.0 copy-start.2
  203.1 0.0 copy-start
  203.1 5.3 %convert_bitcast_fusion = f32[4,24,15,1024]{3,1,2,0:T(8,128)} fusion(bf16[4,15,24,1024]{3,2,1,0:T(8,128)(2,1)} %get-tuple-element.63), kind=kLoop, calls=%fused_computation | loop fusion | flops 1474560 | bytes 8847360 | tf_op jit(solution)/shard_map/transpose | solution.py:1251
  208.4 0.0 copy-done.1
  208.4 0.8 fusion.1
  209.2 0.8 fusion
  210.0 0.0 copy-done.2
  210.0 0.1 constant_dynamic-slice_fusion
  210.1 0.5 slice_bitcast_fusion
  210.7 0.0 copy-done
  210.7 1.6 copy.27
Async XLA Ops:
  203.1 5.3 %copy-start.1 = (f32[64,4096]{1,0:T(8,128)S(1)}, f32[64,4096]{1,0:T(8,128)}, u32[]{:S(2)}) copy-start(f32[64,4096]{1,0:T(8,128)} %get-tuple-element.64) | copy-start | bytes 3145732
  203.1 6.9 %copy-start.2 = (f32[8,128]{1,0:T(8,128)S(1)}, f32[8,128]{1,0:T(8,128)}, u32[]{:S(2)}) copy-start(f32[8,128]{1,0:T(8,128)} %get-tuple-element.65) | copy-start | bytes 12292
  203.1 7.5 %copy-start = (bf16[4,15,24,1024]{3,2,1,0:T(8,128)(2,1)S(1)}, bf16[4,15,24,1024]{3,2,1,0:T(8,128)(2,1)}, u32[]{:S(2)}) copy-start(bf16[4,15,24,1024]{3,2,1,0:T(8,128)(2,1)} %get-tuple-element.51) | copy-start | bytes 8847364

commit v6 on v5

--- a/solution.py
+++ b/solution.py
@@ -20,24 +20,24 @@
 Q, K, V, O, U0, U1, D0, D1 = range(8)
 UPS = (U0, U1)
 DOWNS = (D0, D1)
-ORDERS = ("zxy", "zyx", "zxy", "xyz", "yzx", "zxy", "zyx", "xyz")
-BACK_ORDERS = ("zxy", "xzy", "yxz", "xyz", "xzy", "zxy", "yxz", "xzy", "xzy")
-FEED_ORDERS = ("zxy", "xzy", "zxy", "xzy")
+ORDERS = ("zxy", "zyx", "yxz", "zxy", "zyx", "zxy", "yzx", "xyz")
+BACK_ORDERS = ("zxy", "xzy", "yxz", "xzy", "xyz", "xzy", "yxz", "xzy", "xzy")
+FEED_ORDERS = ("zxy", "zxy", "xzy", "xzy")
 
 FORWARD_PLAN = (
-    0, 1, 4, 3, 0, 8, 2, 7, 3, -1, 0, 1, 0, 8, 7, 1, 2, 1, 8, 8, 2, 2, 5, 6,
-    0, 4, 1, 5, 2, 6, 5, 6, 4, 3, 5, -1, 6, 4, 8, 4, 0, 3, -1, 1, -1, 2, 5, 3,
-    7, -1, -1, -1, 3, 6, -1, -1, -1, 7, -1, 4, -1, 5, -1, 7, -1, 6, -1, -1, 7, -1, -1,
+    0, 1, 2, 3, 7, 0, 8, 6, 1, 2, -1, 0, 8, 0, 3, 7, 1, 4, 8, 3, 1, 8, 6, 5,
+    4, 2, 3, 0, 4, 1, 5, -1, 5, 6, 2, 8, 4, 0, 5, 3, -1, 4, 2, -1, 6, 1, 7, 2,
+    -1, 5, -1, 3, 6, -1, -1, 4, 7, -1, -1, -1, -1, 7, 5, -1, -1, 6, -1, 7, -1, -1, -1,
 )
 FEED_PLAN = (
-    4, -1, 0, 4, -1, 0, 1, -1, 0, 2, 1, 3, -1, 2, -1, 4, -1, 4, 3, 2, 0, -1, -1, 1,
-    -1, 1, 0, 3, 2, -1, 3, -1, 1, 2, 3, 1, 0, -1, 2, 3, -1, 0, 2, 1, 3,
+    4, 4, -1, 0, -1, 1, 0, 4, -1, 2, 3, 4, 1, 3, 0, -1, 2, -1, 1, -1, 0, -1, 3, 1,
+    -1, -1, 2, 0, 3, -1, 1, 0, 2, -1, 3, -1, 2, 1, -1, 3, 2, 1, 3, 0, 2,
 )
 ATTN_PLAN = (
-    2, 0, -1, -1, 2, 1, 0, -1, -1, 1, -1, -1, -1, 0, 4, 6, 5, -1, 8, 5, 6, -1, 10, 8,
-    0, 7, 4, -1, -1, 1, 3, 3, 10, 1, 7, 2, 9, 9, 8, 9, 8, 11, 9, 1, 4, 3, 4, 5,
-    8, 5, 1, 7, 6, 0, 11, 4, 3, 2, 9, 8, 6, 4, 7, 3, 2, 7, 5, 0, 6, 9, 2, 3,
-    5, 6, 7, 1, 4, 8, 0, 5, 2, 3, 7, 6,
+    2, 0, 1, -1, 2, 1, -1, 0, -1, -1, -1, -1, -1, 4, 6, -1, 6, 0, 4, 8, -1, 10, 1, 8,
+    5, 0, 7, 4, 5, 1, -1, 3, 8, 11, 3, 4, 1, 7, 11, 4, 6, 8, 2, -1, 5, 1, 9, 3,
+    9, 9, 10, 9, 5, 3, 7, 7, 5, 6, 6, 8, 0, 1, 5, 3, 2, 7, 9, 2, 8, 3, 0, 4,
+    7, 6, 5, 2, 4, 9, 6, 8, 3, 0, 7, 2,
 )
 GRADS_FIRST = 1
 

time: 212 us -> 213 us (level)
    pallas_call x1, Pallas kernels: 75.8 us -> 78.3 us  [attn_back(): call(functools.partial(attn_back_kernel, shape), tuple(outs), [IN_VMEM] *...]
where the time goes in v6:
time: 213 us
  Pallas kernels  203 us (95%)
  other arithmetic  5.27 us (2%)
  local copies, waits for them, and re-layouts  3.85 us (2%)
    pallas_call x1, Pallas kernels, forward(): call(functools.partial(forward_kernel, shape, micro), (shape_of(full, BF)...  83.5 us
    pallas_call x1, Pallas kernels, attn_back(): call(functools.partial(attn_back_kernel, shape), tuple(outs), [IN_VMEM] *...  78.3 us
    pallas_call x1, Pallas kernels, feed_back(): call(functools.partial(feed_back_kernel, shape), tuple(outs), [IN_VMEM] +...  41.5 us
    transpose x1, other arithmetic, body(): flip = lambda array: jnp.transpose(array, (0, 2, 1, 3))  5.27 us

profile of v6, /device:TPU:0, one launch (start us, length us, event | category | flops | bytes accessed | tf_op | source)
XLA Modules:
  0.0 213.2 jit_solution(3005867827328188649)
XLA Ops:
  0.6 83.5 %forward.1 = (bf16[8,2,4,2,2,64,512]{6,5,4,3,2,1,0:T(8,128)(2,1)}, f32[8,1024]{1,0:T(8,128)}, bf16[768,1024]{1,0:T(8,128)(2,1)}, bf16[768,1024]{1,0:T(8,128)(2,1...) custom-call(bf16[4,15,24,1024]{3,2,1,0:T(8,128)(2,1)} %bitcast.17, ...), custom_call_target="tpu_custom_call" | custom-call | tf_op jit(solution)/shard_map/forward/pallas_call | solution.py:1132
  84.1 41.5 %feed_back.1 = (bf16[5,2,4,2,2,64,512]{6,5,4,3,2,1,0:T(8,128)(2,1)}, f32[768,1024]{1,0:T(8,128)}, bf16[768,1024]{1,0:T(8,128)(2,1)}, f32[2,8,1024]{2,1,0:T(8,128...) custom-call(f32[8,1024]{1,0:T(8,128)} %get-tuple-element.39.vectors, ...), custom_call_target="tpu_custom_call" | custom-call | tf_op jit(solution)/shard_map/feed_back/pallas_call | solution.py:1191
  125.7 78.3 %attn_back.1 = (bf16[4,15,24,1024]{3,2,1,0:T(8,128)(2,1)}, f32[64,4096]{1,0:T(8,128)}, f32[8,128]{1,0:T(8,128)}) custom-call(f32[8,1024]{1,0:T(8,128)} %get-tuple-element.39.vectors, f32[2,8,1024]{2,1,0:T(8,128)} %get-tuple-element.52.vec_f, bf16[8,2,4,2,2,64,512]{6,5,4,3,2,1,0:T(8,128)(2,1)} %get-tuple-element.40.g_in, ...), custom_call_target="tpu_custom_call" | custom-call | tf_op jit(solution)/shard_map/attn_back/pallas_call | solution.py:1225
  204.0 0.0 copy-start.1
  204.0 0.0 copy-start.2
  204.0 0.0 copy-start
  204.0 5.3 %convert_bitcast_fusion = f32[4,24,15,1024]{3,1,2,0:T(8,128)} fusion(bf16[4,15,24,1024]{3,2,1,0:T(8,128)(2,1)} %get-tuple-element.63), kind=kLoop, calls=%fused_computation | loop fusion | flops 1474560 | bytes 8847360 | tf_op jit(solution)/shard_map/transpose | solution.py:1251
  209.3 0.0 copy-done.1
  209.3 0.8 fusion.1
  210.1 0.8 fusion
  210.9 0.0 copy-done.2
  210.9 0.1 constant_dynamic-slice_fusion
  211.0 0.5 slice_bitcast_fusion
  211.5 0.0 copy-done
  211.6 1.6 copy.27
Async XLA Ops:
  204.0 5.3 %copy-start.1 = (f32[64,4096]{1,0:T(8,128)S(1)}, f32[64,4096]{1,0:T(8,128)}, u32[]{:S(2)}) copy-start(f32[64,4096]{1,0:T(8,128)} %get-tuple-element.64) | copy-start | bytes 3145732
  204.0 6.9 %copy-start.2 = (f32[8,128]{1,0:T(8,128)S(1)}, f32[8,128]{1,0:T(8,128)}, u32[]{:S(2)}) copy-start(f32[8,128]{1,0:T(8,128)} %get-tuple-element.65) | copy-start | bytes 12292
  204.0 7.5 %copy-start = (bf16[4,15,24,1024]{3,2,1,0:T(8,128)(2,1)S(1)}, bf16[4,15,24,1024]{3,2,1,0:T(8,128)(2,1)}, u32[]{:S(2)}) copy-start(bf16[4,15,24,1024]{3,2,1,0:T(8,128)(2,1)} %get-tuple-element.51) | copy-start | bytes 8847364

commit v7 on v6

--- a/solution.py
+++ b/solution.py
@@ -21,7 +21,7 @@
 UPS = (U0, U1)
 DOWNS = (D0, D1)
 ORDERS = ("zxy", "zyx", "yxz", "zxy", "zyx", "zxy", "yzx", "xyz")
-BACK_ORDERS = ("zxy", "xzy", "yxz", "xzy", "xyz", "xzy", "yxz", "xzy", "xzy")
+BACK_ORDERS = ("zxy", "xzy", "yxz", "xyz", "xzy", "zxy", "yxz", "xzy", "xzy")
 FEED_ORDERS = ("zxy", "zxy", "xzy", "xzy")
 
 FORWARD_PLAN = (
@@ -34,10 +34,10 @@
     -1, -1, 2, 0, 3, -1, 1, 0, 2, -1, 3, -1, 2, 1, -1, 3, 2, 1, 3, 0, 2,
 )
 ATTN_PLAN = (
-    2, 0, 1, -1, 2, 1, -1, 0, -1, -1, -1, -1, -1, 4, 6, -1, 6, 0, 4, 8, -1, 10, 1, 8,
-    5, 0, 7, 4, 5, 1, -1, 3, 8, 11, 3, 4, 1, 7, 11, 4, 6, 8, 2, -1, 5, 1, 9, 3,
-    9, 9, 10, 9, 5, 3, 7, 7, 5, 6, 6, 8, 0, 1, 5, 3, 2, 7, 9, 2, 8, 3, 0, 4,
-    7, 6, 5, 2, 4, 9, 6, 8, 3, 0, 7, 2,
+    2, 0, -1, -1, 2, 1, 0, -1, -1, 1, -1, -1, -1, 0, 4, 6, 5, -1, 8, 5, 6, -1, 10, 8,
+    0, 7, 4, -1, -1, 1, 3, 3, 10, 1, 7, 2, 9, 9, 8, 9, 8, 11, 9, 1, 4, 3, 4, 5,
+    8, 5, 1, 7, 6, 0, 11, 4, 3, 2, 9, 8, 6, 4, 7, 3, 2, 7, 5, 0, 6, 9, 2, 3,
+    5, 6, 7, 1, 4, 8, 0, 5, 2, 3, 7, 6,
 )
 GRADS_FIRST = 1
 
@@ -801,21 +801,22 @@
         half_out, hands, send, recv, ysem = refs[17:22]
         boxes = list(refs[22:])
         side = mover.start(out_in, half_out)
-    loads = {"glt": mover.start(glt_in, glt), ("active", 0): mover.start(active_in.at[0], active.at[0])}
-    loads["gl"] = mover.start(gl_in, gl)
-    for which in range(2):
-        if which == 1:
-            loads["active", which] = mover.start(active_in.at[which], active.at[which])
-        loads["d", which] = mover.start(g_in.at[DOWNS[which]], g.at[2 + which])
-        loads["slope", which] = mover.start(slope_in.at[which], slope.at[which])
-    loads["nrm2"] = mover.start(nrm2_in, nrm2)
-    for which in range(2):
-        loads["u", which] = mover.start(g_in.at[UPS[which]], g.at[which])
-    loads["res"] = mover.start(res_in, res)
-    loads["cot"] = mover.start(cot_in, cot)
-    loads["mix"] = mover.start(mix_in, mix)
-    loads["o"] = mover.start(g_in.at[O], g.at[4])
-    loads["weight"] = mover.start(weight_in, weight)
+    loads = {}
+
+    def fetch(key, source, target):
+        loads[key] = mover.start(source, target)
+
+    def fetch_down(which):
+        fetch(("active", which), active_in.at[which], active.at[which])
+        fetch(("d", which), g_in.at[DOWNS[which]], g.at[2 + which])
+        fetch(("slope", which), slope_in.at[which], slope.at[which])
+
+    def fetch_up(which):
+        fetch(("u", which), g_in.at[UPS[which]], g.at[which])
+
+    fetch("glt", glt_in, glt)
+    fetch("gl", gl_in, gl)
+    fetch_down(0)
     comm = {}
     if shape:
         place = Place(shape)
@@ -834,7 +835,11 @@
 
     def down_grad(which):
         if which == 0:
+            fetch_down(1)
             loads["glt"].wait()
+        else:
+            fetch_up(1)
+            fetch("res", res_in, res)
         loads["active", which].wait()
         weight_grad(glt, lambda m: active[which, m], dw, 2 + which)
         if not shape:
@@ -842,7 +847,14 @@
 
     def hidden_grad(which):
         if which == 0:
+            fetch("nrm2", nrm2_in, nrm2)
+            fetch_up(0)
             loads["gl"].wait()
+        else:
+            fetch("cot", cot_in, cot)
+            fetch("weight", weight_in, weight)
+            fetch("o", g_in.at[O], g.at[4])
+            fetch("mix", mix_in, mix)
         loads["d", which].wait()
         loads["slope", which].wait()
 
@@ -954,10 +966,7 @@
             loads[name, part] = mover.start(given[name].at[rows], here[name].at[rows])
         if part == 0:
             fetch_held(1, 2)
-    for name in BACK_IN[5:]:
-        loads[name] = mover.start(given[name], here[name])
-    for seg in (Q, K, V):
-        loads[seg] = mover.start(g_in.at[seg], g.at[seg])
+    loads["nrmt"] = mover.start(given["nrmt"], here["nrmt"])
     gm, q, k, v, probs, nrmt, gres, x = (here[name] for name in BACK_IN)
     gn = probs
     if shape:
@@ -1036,6 +1045,10 @@
             vector_tiles(tiles, vec, vec_f)
 
     def before_heads():
+        for seg in (Q, K, V):
+            loads[seg] = mover.start(g_in.at[seg], g.at[seg])
+        for name in ("gres", "x"):
+            loads[name] = mover.start(given[name], here[name])
         loads["nrmt"].wait()
 
     pieces = [ready, (3, mixing, None, None), before_heads]

time: 213 us -> 211 us (level)
    pallas_call x1, Pallas kernels: 78.3 us -> 75.9 us  [attn_back(): call(functools.partial(attn_back_kernel, shape), tuple(outs), [IN_VMEM] *...]
where the time goes in v7:
time: 211 us
  Pallas kernels  201 us (95%)
  other arithmetic  5.27 us (2%)
  local copies, waits for them, and re-layouts  3.85 us (2%)
    pallas_call x1, Pallas kernels, forward(): call(functools.partial(forward_kernel, shape, micro), (shape_of(full, BF)...  83.5 us
    pallas_call x1, Pallas kernels, attn_back(): call(functools.partial(attn_back_kernel, shape), tuple(outs), [IN_VMEM] *...  75.9 us
    pallas_call x1, Pallas kernels, feed_back(): call(functools.partial(feed_back_kernel, shape), tuple(outs), [IN_VMEM] +...  42 us
    transpose x1, other arithmetic, body(): flip = lambda array: jnp.transpose(array, (0, 2, 1, 3))  5.27 us

profile of v7, /device:TPU:0, one launch (start us, length us, event | category | flops | bytes accessed | tf_op | source)
XLA Modules:
  0.0 211.1 jit_solution(5927541451395302349)
XLA Ops:
  0.6 83.5 %forward.1 = (bf16[8,2,4,2,2,64,512]{6,5,4,3,2,1,0:T(8,128)(2,1)}, f32[8,1024]{1,0:T(8,128)}, bf16[768,1024]{1,0:T(8,128)(2,1)}, bf16[768,1024]{1,0:T(8,128)(2,1...) custom-call(bf16[4,15,24,1024]{3,2,1,0:T(8,128)(2,1)} %bitcast.17, ...), custom_call_target="tpu_custom_call" | custom-call | tf_op jit(solution)/shard_map/forward/pallas_call | solution.py:1145
  84.1 42.0 %feed_back.1 = (bf16[5,2,4,2,2,64,512]{6,5,4,3,2,1,0:T(8,128)(2,1)}, f32[768,1024]{1,0:T(8,128)}, bf16[768,1024]{1,0:T(8,128)(2,1)}, f32[2,8,1024]{2,1,0:T(8,128...) custom-call(f32[8,1024]{1,0:T(8,128)} %get-tuple-element.39.vectors, ...), custom_call_target="tpu_custom_call" | custom-call | tf_op jit(solution)/shard_map/feed_back/pallas_call | solution.py:1204
  126.1 75.9 %attn_back.1 = (bf16[4,15,24,1024]{3,2,1,0:T(8,128)(2,1)}, f32[64,4096]{1,0:T(8,128)}, f32[8,128]{1,0:T(8,128)}) custom-call(f32[8,1024]{1,0:T(8,128)} %get-tuple-element.39.vectors, f32[2,8,1024]{2,1,0:T(8,128)} %get-tuple-element.52.vec_f, bf16[8,2,4,2,2,64,512]{6,5,4,3,2,1,0:T(8,128)(2,1)} %get-tuple-element.40.g_in, ...), custom_call_target="tpu_custom_call" | custom-call | tf_op jit(solution)/shard_map/attn_back/pallas_call | solution.py:1238
  202.0 0.0 copy-start.1
  202.0 0.0 copy-start.2
  202.0 0.0 copy-start
  202.0 5.3 %convert_bitcast_fusion = f32[4,24,15,1024]{3,1,2,0:T(8,128)} fusion(bf16[4,15,24,1024]{3,2,1,0:T(8,128)(2,1)} %get-tuple-element.63), kind=kLoop, calls=%fused_computation | loop fusion | flops 1474560 | bytes 8847360 | tf_op jit(solution)/shard_map/transpose | solution.py:1264
  207.3 0.0 copy-done.1
  207.3 0.8 fusion.1
  208.1 0.8 fusion
  208.9 0.0 copy-done.2
  208.9 0.1 constant_dynamic-slice_fusion
  209.0 0.5 slice_bitcast_fusion
  209.5 0.0 copy-done
  209.5 1.6 copy.27
Async XLA Ops:
  202.0 5.3 %copy-start.1 = (f32[64,4096]{1,0:T(8,128)S(1)}, f32[64,4096]{1,0:T(8,128)}, u32[]{:S(2)}) copy-start(f32[64,4096]{1,0:T(8,128)} %get-tuple-element.64) | copy-start | bytes 3145732
  202.0 6.9 %copy-start.2 = (f32[8,128]{1,0:T(8,128)S(1)}, f32[8,128]{1,0:T(8,128)}, u32[]{:S(2)}) copy-start(f32[8,128]{1,0:T(8,128)} %get-tuple-element.65) | copy-start | bytes 12292
  202.0 7.5 %copy-start = (bf16[4,15,24,1024]{3,2,1,0:T(8,128)(2,1)S(1)}, bf16[4,15,24,1024]{3,2,1,0:T(8,128)(2,1)}, u32[]{:S(2)}) copy-start(bf16[4,15,24,1024]{3,2,1,0:T(8,128)(2,1)} %get-tuple-element.51) | copy-start | bytes 8847364
